TPU v7x, 256 devices: a whole 4x4x8 slice. The times are simulated.
256 devices in a mesh: dp: 16 (over z, x_hi), pipe: 4 (over y), tensor: 4 (over x_lo, core).
Axes of the slice: x: 4 (x_hi: 2, x_lo: 2; x = x_hi * 2 + x_lo), y: 4, z: 8, core: 2. Of those that a mesh axis runs over, the one named last changes fastest.
Arguments:
- grad_out: bfloat16 [8, 1024, 4096], P(None, 'dp', 'tensor'), may hold values from -6 to 6
- activations: bfloat16 [4, 3, 8, 1024, 4096], P('pipe', None, None, 'dp', 'tensor'), may hold values from -6 to 6
- mixing: bfloat16 [4, 3, 32, 128, 128], P('pipe', None, 'tensor'), may hold values from -0.1875 to 0.1875
- proj_tiles: bfloat16 [4, 3, 8, 128, 128], P('pipe'), may hold values from -0.1875 to 0.1875
- proj_blocks: int32 [4, 3, 8], P('pipe'), may hold values from 0 to 31, all different within a row
- section_sizes: int32 [4], replicated, may hold values from 1 to 3, 8 in all
Outputs:
- segment_grads: bfloat16 [4, 8, 1024, 4096], P('pipe', None, 'dp', 'tensor')
- sketches: float32 [4, 3, 8, 4096], P('pipe')
Inputs may be any that keep to these rules, and one draw needn't show every extreme that they name: `section_sizes`: each segment holds 1 to 3 layers, 8 in all, some segment exactly 3. `proj_blocks`: the 8 blocks of one slot are distinct.
All inputs are finite; a program needn't handle non-finite values.
Results may differ from a plain program's by a relative error of at most 0.0074.
Values may be sent and summed in bfloat16 or wider, within the bound.
A program may use at most 64 MiB of HBM per device.

v0:
```python
import math

import jax
import jax.numpy as jnp
from jax import lax
from jax.sharding import PartitionSpec as P


def shifted(x, axis, by):
    peers = lax.axis_size(axis)
    pairs = [(i, i + by) for i in range(peers) if 0 <= i + by < peers]
    return lax.ppermute(x, axis, pairs)


def silu_slope(value):
    sig = jax.nn.sigmoid(value)
    return sig * (1.0 + value * (1.0 - sig))


def shards(grad_out, activations, mixing, proj_tiles, proj_blocks, section_sizes):
    high = lax.Precision.HIGHEST
    segments = lax.axis_size("pipe")
    segment = lax.axis_index("pipe")
    half = lax.axis_index("tensor")
    micro = grad_out.shape[0]
    tokens = grad_out.shape[1]
    local_width = grad_out.shape[2]
    slots = activations.shape[1]
    heads_local = mixing.shape[2]
    head_size = mixing.shape[3]
    rank = proj_tiles.shape[4] // 2
    scale = 1.0 / math.sqrt(tokens * lax.axis_size("dp"))
    live_count = section_sizes[segment]
    owned = heads_local * half + jnp.arange(heads_local, dtype=jnp.int32)
    select = (proj_blocks[0][:, :, None] == owned[None, None, :]).astype(jnp.bfloat16)
    dense = jnp.einsum("kjb,kjcr->kbcr", select, proj_tiles[0], preferred_element_type=jnp.float32)
    dense = dense.astype(jnp.bfloat16).reshape(slots, heads_local * head_size, 2 * rank)
    live_slots = jnp.arange(slots, dtype=jnp.int32) < live_count

    def process(grad, start, width):
        acts = lax.dynamic_slice_in_dim(activations[0], start, width, 1)
        act_parts = [None] * slots
        delta_parts = [None] * slots
        for slot in range(slots - 1, -1, -1):
            flat_act = acts[slot].reshape(width * tokens, local_width)
            heads_in = acts[slot].reshape(width, tokens, heads_local, head_size)
            pre = jnp.einsum(
                "mthc,hcd->mthd", heads_in, mixing[0, slot], preferred_element_type=jnp.float32
            )
            grad_heads = grad.reshape(width, tokens, heads_local, head_size).astype(jnp.float32)
            delta = (grad_heads * silu_slope(pre)).astype(jnp.bfloat16)
            back = jnp.einsum(
                "mthd,hcd->mthc", delta, mixing[0, slot], preferred_element_type=jnp.float32
            )
            moved = (grad_heads + back).reshape(width, tokens, local_width).astype(jnp.bfloat16)
            grad = jnp.where(slot < live_count, moved, grad)
            act_parts[slot] = jnp.dot(
                flat_act, dense[slot, :, :rank], preferred_element_type=jnp.float32
            )
            delta_parts[slot] = jnp.dot(
                delta.reshape(width * tokens, local_width),
                dense[slot, :, rank:],
                preferred_element_type=jnp.float32,
            )
        act_proj, grad_proj = lax.psum((jnp.stack(act_parts), jnp.stack(delta_parts)), "tensor")
        act_proj = act_proj.reshape(slots, width, tokens, rank)
        grad_proj = grad_proj.reshape(slots, width, tokens, rank)
        sketch = jnp.einsum("kmtr,kmts->kmrs", grad_proj, act_proj, precision=high) * scale
        sketch = jnp.where(live_slots[:, None, None, None], sketch, 0.0).reshape(
            slots, width, rank * rank
        )
        return (grad, sketch)

    width = 1
    groups = micro // width
    turns = groups + segments - 1

    def turn(step, carry):
        incoming, segment_out, sketches = carry
        group = step - (segments - 1 - segment)
        valid = jnp.logical_and(group >= 0, group < groups)
        start = jnp.clip(group, 0, groups - 1) * width
        top = lax.dynamic_slice_in_dim(grad_out, start, width, 0)
        grad = jnp.where(segment == segments - 1, top, incoming)
        grad, sketch = process(grad, start, width)
        sketch = lax.psum(sketch, "dp")
        old_out = lax.dynamic_slice_in_dim(segment_out, start, width, 0)
        segment_out = lax.dynamic_update_slice_in_dim(
            segment_out, jnp.where(valid, grad, old_out), start, 0
        )
        old_sketch = lax.dynamic_slice_in_dim(sketches, start, width, 1)
        sketches = lax.dynamic_update_slice_in_dim(
            sketches, jnp.where(valid, sketch, old_sketch), start, 1
        )
        incoming = shifted(grad, "pipe", -1)
        return (incoming, segment_out, sketches)

    start_carry = (
        jnp.zeros((width, tokens, local_width), jnp.bfloat16),
        jnp.zeros_like(grad_out),
        jnp.zeros((slots, micro, rank * rank), jnp.float32),
    )
    incoming, segment_out, sketches = lax.fori_loop(0, turns, turn, start_carry)
    return (segment_out[None], sketches[None])


def solution(mesh):
    return jax.shard_map(
        shards,
        mesh=mesh,
        in_specs=(
            P(None, "dp", "tensor"),
            P("pipe", None, None, "dp", "tensor"),
            P("pipe", None, "tensor", None, None),
            P("pipe", None, None, None, None),
            P("pipe", None, None),
            P(),
        ),
        out_specs=(P("pipe", None, "dp", "tensor"), P("pipe", None, None, None)),
        check_vma=False,
    )
```

profile of v0, /device:TPU:1, one launch (start us, length us, event | category | flops | bytes accessed | tf_op | source)
XLA Modules:
  0.0 1450.4 jit_solution(14424018004752751403)
XLA Ops:
  7.2 1.4 dynamic_slice.35
  12.2 1.1 broadcast_in_dim.40
  13.3 1429.7 %while.20 = (s32[]{:T(128)}, bf16[1,64,1024]{2,1,0:T(8,128)(2,1)S(1)}, bf16[8,64,1024]{2,1,0:T(8,128)(2,1)}, f32[3,8,4096]{2,1,0:T(8,128)S(1)}, pred[]{:T(512)},...) while((s32[]{:T(128)}, ...), condition=%wide.region_4.5_spmd.clone, body=%wide.region_0.4_spmd.clone.sunk | while | flops 163307520 | bytes 16024470 | solution.py:103
  17.3 1.6 select_dynamic-update-slice_fusion.2
  19.0 1.3 collective-permute-start
  20.3 1.1 convolution_bitcast_fusion.22
  26.7 46.1 %all-reduce.5.cloned.1.call-done = (f32[3,64,64]{2,1,0:T(8,128)}, f32[3,64,64]{2,1,0:T(8,128)}) async-done(((f32[3,64,64]{2,1,0:T(8,128)}, f32[3,64,64]{2,1,0:T(8,128)}), (f32[3,64,64]{2,1,0:T(8,128)}, f32[3,64,64]{2,1,0:T(8,128)})) %all-reduce.5.cloned.1.call-update) | async-done | bytes 98320 | tf_op jit(solution)/shard_map/while/body/eval_jaxpr/psum | solution.py:65
  72.8 1.3 fusion.129
  74.2 63.1 %psum.43 = f32[3,1,4096]{2,0,1:T(4,128)S(1)} all-reduce(f32[3,1,4096]{2,0,1:T(4,128)S(1)} %reshape.292), channel_id=1, replica_groups=mesh['dp'=16,'pipe'=4,'tensor'=4] {'dp'}, use_global_device_ids=true, to_apply=%region_3.3 | all-reduce | flops 12288 | bytes 98304 | tf_op jit(solution)/shard_map/while/body/eval_jaxpr/psum | solution.py:86
  141.9 1.6 select_dynamic-update-slice_fusion.2
  143.5 1.3 collective-permute-start
  144.8 1.1 convolution_bitcast_fusion.22
  151.3 52.0 %all-reduce.5.cloned.1.call-done = (f32[3,64,64]{2,1,0:T(8,128)}, f32[3,64,64]{2,1,0:T(8,128)}) async-done(((f32[3,64,64]{2,1,0:T(8,128)}, f32[3,64,64]{2,1,0:T(8,128)}), (f32[3,64,64]{2,1,0:T(8,128)}, f32[3,64,64]{2,1,0:T(8,128)})) %all-reduce.5.cloned.1.call-update) | async-done | bytes 98320 | tf_op jit(solution)/shard_map/while/body/eval_jaxpr/psum | solution.py:65
  203.4 1.3 fusion.129
  204.7 63.1 %psum.43 = f32[3,1,4096]{2,0,1:T(4,128)S(1)} all-reduce(f32[3,1,4096]{2,0,1:T(4,128)S(1)} %reshape.292), channel_id=1, replica_groups=mesh['dp'=16,'pipe'=4,'tensor'=4] {'dp'}, use_global_device_ids=true, to_apply=%region_3.3 | all-reduce | flops 12288 | bytes 98304 | tf_op jit(solution)/shard_map/while/body/eval_jaxpr/psum | solution.py:86
  272.4 1.6 select_dynamic-update-slice_fusion.2
  274.0 1.3 collective-permute-start
  275.3 1.1 convolution_bitcast_fusion.22
  281.8 52.1 %all-reduce.5.cloned.1.call-done = (f32[3,64,64]{2,1,0:T(8,128)}, f32[3,64,64]{2,1,0:T(8,128)}) async-done(((f32[3,64,64]{2,1,0:T(8,128)}, f32[3,64,64]{2,1,0:T(8,128)}), (f32[3,64,64]{2,1,0:T(8,128)}, f32[3,64,64]{2,1,0:T(8,128)})) %all-reduce.5.cloned.1.call-update) | async-done | bytes 98320 | tf_op jit(solution)/shard_map/while/body/eval_jaxpr/psum | solution.py:65
  333.9 1.3 fusion.129
  335.3 63.1 %psum.43 = f32[3,1,4096]{2,0,1:T(4,128)S(1)} all-reduce(f32[3,1,4096]{2,0,1:T(4,128)S(1)} %reshape.292), channel_id=1, replica_groups=mesh['dp'=16,'pipe'=4,'tensor'=4] {'dp'}, use_global_device_ids=true, to_apply=%region_3.3 | all-reduce | flops 12288 | bytes 98304 | tf_op jit(solution)/shard_map/while/body/eval_jaxpr/psum | solution.py:86
  403.0 1.6 select_dynamic-update-slice_fusion.2
  404.6 1.3 collective-permute-start
  405.9 1.1 convolution_bitcast_fusion.22
  412.4 52.1 %all-reduce.5.cloned.1.call-done = (f32[3,64,64]{2,1,0:T(8,128)}, f32[3,64,64]{2,1,0:T(8,128)}) async-done(((f32[3,64,64]{2,1,0:T(8,128)}, f32[3,64,64]{2,1,0:T(8,128)}), (f32[3,64,64]{2,1,0:T(8,128)}, f32[3,64,64]{2,1,0:T(8,128)})) %all-reduce.5.cloned.1.call-update) | async-done | bytes 98320 | tf_op jit(solution)/shard_map/while/body/eval_jaxpr/psum | solution.py:65
  464.4 1.3 fusion.129
  465.8 63.1 %psum.43 = f32[3,1,4096]{2,0,1:T(4,128)S(1)} all-reduce(f32[3,1,4096]{2,0,1:T(4,128)S(1)} %reshape.292), channel_id=1, replica_groups=mesh['dp'=16,'pipe'=4,'tensor'=4] {'dp'}, use_global_device_ids=true, to_apply=%region_3.3 | all-reduce | flops 12288 | bytes 98304 | tf_op jit(solution)/shard_map/while/body/eval_jaxpr/psum | solution.py:86
  533.5 1.6 select_dynamic-update-slice_fusion.2
  535.1 1.3 collective-permute-start
  536.4 1.1 convolution_bitcast_fusion.22
  542.9 52.1 %all-reduce.5.cloned.1.call-done = (f32[3,64,64]{2,1,0:T(8,128)}, f32[3,64,64]{2,1,0:T(8,128)}) async-done(((f32[3,64,64]{2,1,0:T(8,128)}, f32[3,64,64]{2,1,0:T(8,128)}), (f32[3,64,64]{2,1,0:T(8,128)}, f32[3,64,64]{2,1,0:T(8,128)})) %all-reduce.5.cloned.1.call-update) | async-done | bytes 98320 | tf_op jit(solution)/shard_map/while/body/eval_jaxpr/psum | solution.py:65
  594.9 1.3 fusion.129
  596.3 63.1 %psum.43 = f32[3,1,4096]{2,0,1:T(4,128)S(1)} all-reduce(f32[3,1,4096]{2,0,1:T(4,128)S(1)} %reshape.292), channel_id=1, replica_groups=mesh['dp'=16,'pipe'=4,'tensor'=4] {'dp'}, use_global_device_ids=true, to_apply=%region_3.3 | all-reduce | flops 12288 | bytes 98304 | tf_op jit(solution)/shard_map/while/body/eval_jaxpr/psum | solution.py:86
  664.0 1.6 select_dynamic-update-slice_fusion.2
  665.6 1.3 collective-permute-start
  673.4 52.1 %all-reduce.5.cloned.1.call-done = (f32[3,64,64]{2,1,0:T(8,128)}, f32[3,64,64]{2,1,0:T(8,128)}) async-done(((f32[3,64,64]{2,1,0:T(8,128)}, f32[3,64,64]{2,1,0:T(8,128)}), (f32[3,64,64]{2,1,0:T(8,128)}, f32[3,64,64]{2,1,0:T(8,128)})) %all-reduce.5.cloned.1.call-update) | async-done | bytes 98320 | tf_op jit(solution)/shard_map/while/body/eval_jaxpr/psum | solution.py:65
  725.5 1.3 fusion.129
  726.8 63.1 %psum.43 = f32[3,1,4096]{2,0,1:T(4,128)S(1)} all-reduce(f32[3,1,4096]{2,0,1:T(4,128)S(1)} %reshape.292), channel_id=1, replica_groups=mesh['dp'=16,'pipe'=4,'tensor'=4] {'dp'}, use_global_device_ids=true, to_apply=%region_3.3 | all-reduce | flops 12288 | bytes 98304 | tf_op jit(solution)/shard_map/while/body/eval_jaxpr/psum | solution.py:86
  794.5 1.6 select_dynamic-update-slice_fusion.2
  796.2 1.3 collective-permute-start
  803.9 52.1 %all-reduce.5.cloned.1.call-done = (f32[3,64,64]{2,1,0:T(8,128)}, f32[3,64,64]{2,1,0:T(8,128)}) async-done(((f32[3,64,64]{2,1,0:T(8,128)}, f32[3,64,64]{2,1,0:T(8,128)}), (f32[3,64,64]{2,1,0:T(8,128)}, f32[3,64,64]{2,1,0:T(8,128)})) %all-reduce.5.cloned.1.call-update) | async-done | bytes 98320 | tf_op jit(solution)/shard_map/while/body/eval_jaxpr/psum | solution.py:65
  856.0 1.3 fusion.129
  857.4 63.1 %psum.43 = f32[3,1,4096]{2,0,1:T(4,128)S(1)} all-reduce(f32[3,1,4096]{2,0,1:T(4,128)S(1)} %reshape.292), channel_id=1, replica_groups=mesh['dp'=16,'pipe'=4,'tensor'=4] {'dp'}, use_global_device_ids=true, to_apply=%region_3.3 | all-reduce | flops 12288 | bytes 98304 | tf_op jit(solution)/shard_map/while/body/eval_jaxpr/psum | solution.py:86
  925.1 1.6 select_dynamic-update-slice_fusion.2
  926.7 1.3 collective-permute-start
  934.5 52.1 %all-reduce.5.cloned.1.call-done = (f32[3,64,64]{2,1,0:T(8,128)}, f32[3,64,64]{2,1,0:T(8,128)}) async-done(((f32[3,64,64]{2,1,0:T(8,128)}, f32[3,64,64]{2,1,0:T(8,128)}), (f32[3,64,64]{2,1,0:T(8,128)}, f32[3,64,64]{2,1,0:T(8,128)})) %all-reduce.5.cloned.1.call-update) | async-done | bytes 98320 | tf_op jit(solution)/shard_map/while/body/eval_jaxpr/psum | solution.py:65
  986.5 1.3 fusion.129
  987.9 63.1 %psum.43 = f32[3,1,4096]{2,0,1:T(4,128)S(1)} all-reduce(f32[3,1,4096]{2,0,1:T(4,128)S(1)} %reshape.292), channel_id=1, replica_groups=mesh['dp'=16,'pipe'=4,'tensor'=4] {'dp'}, use_global_device_ids=true, to_apply=%region_3.3 | all-reduce | flops 12288 | bytes 98304 | tf_op jit(solution)/shard_map/while/body/eval_jaxpr/psum | solution.py:86
  1055.6 1.6 select_dynamic-update-slice_fusion.2
  1057.2 1.3 collective-permute-start
  1058.5 1.1 convolution_bitcast_fusion.22
  1065.0 52.1 %all-reduce.5.cloned.1.call-done = (f32[3,64,64]{2,1,0:T(8,128)}, f32[3,64,64]{2,1,0:T(8,128)}) async-done(((f32[3,64,64]{2,1,0:T(8,128)}, f32[3,64,64]{2,1,0:T(8,128)}), (f32[3,64,64]{2,1,0:T(8,128)}, f32[3,64,64]{2,1,0:T(8,128)})) %all-reduce.5.cloned.1.call-update) | async-done | bytes 98320 | tf_op jit(solution)/shard_map/while/body/eval_jaxpr/psum | solution.py:65
  1117.0 1.3 fusion.129
  1118.4 63.1 %psum.43 = f32[3,1,4096]{2,0,1:T(4,128)S(1)} all-reduce(f32[3,1,4096]{2,0,1:T(4,128)S(1)} %reshape.292), channel_id=1, replica_groups=mesh['dp'=16,'pipe'=4,'tensor'=4] {'dp'}, use_global_device_ids=true, to_apply=%region_3.3 | all-reduce | flops 12288 | bytes 98304 | tf_op jit(solution)/shard_map/while/body/eval_jaxpr/psum | solution.py:86
  1186.1 1.6 select_dynamic-update-slice_fusion.2
  1187.7 1.3 collective-permute-start
  1195.5 52.1 %all-reduce.5.cloned.1.call-done = (f32[3,64,64]{2,1,0:T(8,128)}, f32[3,64,64]{2,1,0:T(8,128)}) async-done(((f32[3,64,64]{2,1,0:T(8,128)}, f32[3,64,64]{2,1,0:T(8,128)}), (f32[3,64,64]{2,1,0:T(8,128)}, f32[3,64,64]{2,1,0:T(8,128)})) %all-reduce.5.cloned.1.call-update) | async-done | bytes 98320 | tf_op jit(solution)/shard_map/while/body/eval_jaxpr/psum | solution.py:65
  1247.6 1.3 fusion.129
  1248.9 63.1 %psum.43 = f32[3,1,4096]{2,0,1:T(4,128)S(1)} all-reduce(f32[3,1,4096]{2,0,1:T(4,128)S(1)} %reshape.292), channel_id=1, replica_groups=mesh['dp'=16,'pipe'=4,'tensor'=4] {'dp'}, use_global_device_ids=true, to_apply=%region_3.3 | all-reduce | flops 12288 | bytes 98304 | tf_op jit(solution)/shard_map/while/body/eval_jaxpr/psum | solution.py:86
  1316.6 1.6 select_dynamic-update-slice_fusion.2
  1318.3 1.3 collective-permute-start
  1326.0 52.1 %all-reduce.5.cloned.1.call-done = (f32[3,64,64]{2,1,0:T(8,128)}, f32[3,64,64]{2,1,0:T(8,128)}) async-done(((f32[3,64,64]{2,1,0:T(8,128)}, f32[3,64,64]{2,1,0:T(8,128)}), (f32[3,64,64]{2,1,0:T(8,128)}, f32[3,64,64]{2,1,0:T(8,128)})) %all-reduce.5.cloned.1.call-update) | async-done | bytes 98320 | tf_op jit(solution)/shard_map/while/body/eval_jaxpr/psum | solution.py:65
  1378.1 1.3 fusion.129
  1379.5 63.1 %psum.43 = f32[3,1,4096]{2,0,1:T(4,128)S(1)} all-reduce(f32[3,1,4096]{2,0,1:T(4,128)S(1)} %reshape.292), channel_id=1, replica_groups=mesh['dp'=16,'pipe'=4,'tensor'=4] {'dp'}, use_global_device_ids=true, to_apply=%region_3.3 | all-reduce | flops 12288 | bytes 98304 | tf_op jit(solution)/shard_map/while/body/eval_jaxpr/psum | solution.py:86
  (402 shorter events, 116.4 us)
Async XLA Ops:
  7.2 3.6 copy-start
  7.2 6.1 copy-start.1
  13.3 59.5 %all-reduce.5.cloned.1.call-start = ((), (), s32[]{:S(2)}) async-start(), calls=%async_computation | async-start | bytes 393216 | tf_op jit(solution)/shard_map/while/body/eval_jaxpr/psum | solution.py:65
  19.0 118.8 %collective-permute-start = (bf16[1,64,1024]{2,1,0:T(8,128)(2,1)S(1)}, bf16[1,64,1024]{2,1,0:T(8,128)(2,1)S(1)}, u32[]{:S(2)}, u32[]{:S(2)}) collective-permute-start(bf16[1,64,1024]{2,1,0:T(8,128)(2,1)S(1)} %get-tuple-element.449), channel_id=1, source_target_pairs={{4,0},{8,4},{12,8},{5,1},{9,5},{13,9},{6,2},{10,6},{14,10},{7,3},{... | collective-permute-start | bytes 393224 | tf_op jit(solution)/shard_map/while/body/eval_jaxpr/ppermute | solution.py:12
  137.8 65.5 %all-reduce.5.cloned.1.call-start = ((), (), s32[]{:S(2)}) async-start(), calls=%async_computation | async-start | bytes 393216 | tf_op jit(solution)/shard_map/while/body/eval_jaxpr/psum | solution.py:65
  143.5 124.8 %collective-permute-start = (bf16[1,64,1024]{2,1,0:T(8,128)(2,1)S(1)}, bf16[1,64,1024]{2,1,0:T(8,128)(2,1)S(1)}, u32[]{:S(2)}, u32[]{:S(2)}) collective-permute-start(bf16[1,64,1024]{2,1,0:T(8,128)(2,1)S(1)} %get-tuple-element.449), channel_id=1, source_target_pairs={{4,0},{8,4},{12,8},{5,1},{9,5},{13,9},{6,2},{10,6},{14,10},{7,3},{... | collective-permute-start | bytes 393224 | tf_op jit(solution)/shard_map/while/body/eval_jaxpr/ppermute | solution.py:12
  268.3 65.5 %all-reduce.5.cloned.1.call-start = ((), (), s32[]{:S(2)}) async-start(), calls=%async_computation | async-start | bytes 393216 | tf_op jit(solution)/shard_map/while/body/eval_jaxpr/psum | solution.py:65
  274.0 124.8 %collective-permute-start = (bf16[1,64,1024]{2,1,0:T(8,128)(2,1)S(1)}, bf16[1,64,1024]{2,1,0:T(8,128)(2,1)S(1)}, u32[]{:S(2)}, u32[]{:S(2)}) collective-permute-start(bf16[1,64,1024]{2,1,0:T(8,128)(2,1)S(1)} %get-tuple-element.449), channel_id=1, source_target_pairs={{4,0},{8,4},{12,8},{5,1},{9,5},{13,9},{6,2},{10,6},{14,10},{7,3},{... | collective-permute-start | bytes 393224 | tf_op jit(solution)/shard_map/while/body/eval_jaxpr/ppermute | solution.py:12
  398.9 65.5 %all-reduce.5.cloned.1.call-start = ((), (), s32[]{:S(2)}) async-start(), calls=%async_computation | async-start | bytes 393216 | tf_op jit(solution)/shard_map/while/body/eval_jaxpr/psum | solution.py:65
  404.6 124.8 %collective-permute-start = (bf16[1,64,1024]{2,1,0:T(8,128)(2,1)S(1)}, bf16[1,64,1024]{2,1,0:T(8,128)(2,1)S(1)}, u32[]{:S(2)}, u32[]{:S(2)}) collective-permute-start(bf16[1,64,1024]{2,1,0:T(8,128)(2,1)S(1)} %get-tuple-element.449), channel_id=1, source_target_pairs={{4,0},{8,4},{12,8},{5,1},{9,5},{13,9},{6,2},{10,6},{14,10},{7,3},{... | collective-permute-start | bytes 393224 | tf_op jit(solution)/shard_map/while/body/eval_jaxpr/ppermute | solution.py:12
  529.4 65.5 %all-reduce.5.cloned.1.call-start = ((), (), s32[]{:S(2)}) async-start(), calls=%async_computation | async-start | bytes 393216 | tf_op jit(solution)/shard_map/while/body/eval_jaxpr/psum | solution.py:65
  535.1 124.8 %collective-permute-start = (bf16[1,64,1024]{2,1,0:T(8,128)(2,1)S(1)}, bf16[1,64,1024]{2,1,0:T(8,128)(2,1)S(1)}, u32[]{:S(2)}, u32[]{:S(2)}) collective-permute-start(bf16[1,64,1024]{2,1,0:T(8,128)(2,1)S(1)} %get-tuple-element.449), channel_id=1, source_target_pairs={{4,0},{8,4},{12,8},{5,1},{9,5},{13,9},{6,2},{10,6},{14,10},{7,3},{... | collective-permute-start | bytes 393224 | tf_op jit(solution)/shard_map/while/body/eval_jaxpr/ppermute | solution.py:12
  659.9 65.5 %all-reduce.5.cloned.1.call-start = ((), (), s32[]{:S(2)}) async-start(), calls=%async_computation | async-start | bytes 393216 | tf_op jit(solution)/shard_map/while/body/eval_jaxpr/psum | solution.py:65
  665.6 124.8 %collective-permute-start = (bf16[1,64,1024]{2,1,0:T(8,128)(2,1)S(1)}, bf16[1,64,1024]{2,1,0:T(8,128)(2,1)S(1)}, u32[]{:S(2)}, u32[]{:S(2)}) collective-permute-start(bf16[1,64,1024]{2,1,0:T(8,128)(2,1)S(1)} %get-tuple-element.449), channel_id=1, source_target_pairs={{4,0},{8,4},{12,8},{5,1},{9,5},{13,9},{6,2},{10,6},{14,10},{7,3},{... | collective-permute-start | bytes 393224 | tf_op jit(solution)/shard_map/while/body/eval_jaxpr/ppermute | solution.py:12
  790.4 65.5 %all-reduce.5.cloned.1.call-start = ((), (), s32[]{:S(2)}) async-start(), calls=%async_computation | async-start | bytes 393216 | tf_op jit(solution)/shard_map/while/body/eval_jaxpr/psum | solution.py:65
  796.2 124.8 %collective-permute-start = (bf16[1,64,1024]{2,1,0:T(8,128)(2,1)S(1)}, bf16[1,64,1024]{2,1,0:T(8,128)(2,1)S(1)}, u32[]{:S(2)}, u32[]{:S(2)}) collective-permute-start(bf16[1,64,1024]{2,1,0:T(8,128)(2,1)S(1)} %get-tuple-element.449), channel_id=1, source_target_pairs={{4,0},{8,4},{12,8},{5,1},{9,5},{13,9},{6,2},{10,6},{14,10},{7,3},{... | collective-permute-start | bytes 393224 | tf_op jit(solution)/shard_map/while/body/eval_jaxpr/ppermute | solution.py:12
  921.0 65.5 %all-reduce.5.cloned.1.call-start = ((), (), s32[]{:S(2)}) async-start(), calls=%async_computation | async-start | bytes 393216 | tf_op jit(solution)/shard_map/while/body/eval_jaxpr/psum | solution.py:65
  926.7 124.8 %collective-permute-start = (bf16[1,64,1024]{2,1,0:T(8,128)(2,1)S(1)}, bf16[1,64,1024]{2,1,0:T(8,128)(2,1)S(1)}, u32[]{:S(2)}, u32[]{:S(2)}) collective-permute-start(bf16[1,64,1024]{2,1,0:T(8,128)(2,1)S(1)} %get-tuple-element.449), channel_id=1, source_target_pairs={{4,0},{8,4},{12,8},{5,1},{9,5},{13,9},{6,2},{10,6},{14,10},{7,3},{... | collective-permute-start | bytes 393224 | tf_op jit(solution)/shard_map/while/body/eval_jaxpr/ppermute | solution.py:12
  1051.5 65.5 %all-reduce.5.cloned.1.call-start = ((), (), s32[]{:S(2)}) async-start(), calls=%async_computation | async-start | bytes 393216 | tf_op jit(solution)/shard_map/while/body/eval_jaxpr/psum | solution.py:65
  1057.2 124.8 %collective-permute-start = (bf16[1,64,1024]{2,1,0:T(8,128)(2,1)S(1)}, bf16[1,64,1024]{2,1,0:T(8,128)(2,1)S(1)}, u32[]{:S(2)}, u32[]{:S(2)}) collective-permute-start(bf16[1,64,1024]{2,1,0:T(8,128)(2,1)S(1)} %get-tuple-element.449), channel_id=1, source_target_pairs={{4,0},{8,4},{12,8},{5,1},{9,5},{13,9},{6,2},{10,6},{14,10},{7,3},{... | collective-permute-start | bytes 393224 | tf_op jit(solution)/shard_map/while/body/eval_jaxpr/ppermute | solution.py:12
  1182.0 65.5 %all-reduce.5.cloned.1.call-start = ((), (), s32[]{:S(2)}) async-start(), calls=%async_computation | async-start | bytes 393216 | tf_op jit(solution)/shard_map/while/body/eval_jaxpr/psum | solution.py:65
  1187.7 124.8 %collective-permute-start = (bf16[1,64,1024]{2,1,0:T(8,128)(2,1)S(1)}, bf16[1,64,1024]{2,1,0:T(8,128)(2,1)S(1)}, u32[]{:S(2)}, u32[]{:S(2)}) collective-permute-start(bf16[1,64,1024]{2,1,0:T(8,128)(2,1)S(1)} %get-tuple-element.449), channel_id=1, source_target_pairs={{4,0},{8,4},{12,8},{5,1},{9,5},{13,9},{6,2},{10,6},{14,10},{7,3},{... | collective-permute-start | bytes 393224 | tf_op jit(solution)/shard_map/while/body/eval_jaxpr/ppermute | solution.py:12
  1312.6 65.5 %all-reduce.5.cloned.1.call-start = ((), (), s32[]{:S(2)}) async-start(), calls=%async_computation | async-start | bytes 393216 | tf_op jit(solution)/shard_map/while/body/eval_jaxpr/psum | solution.py:65
  1318.3 124.8 %collective-permute-start = (bf16[1,64,1024]{2,1,0:T(8,128)(2,1)S(1)}, bf16[1,64,1024]{2,1,0:T(8,128)(2,1)S(1)}, u32[]{:S(2)}, u32[]{:S(2)}) collective-permute-start(bf16[1,64,1024]{2,1,0:T(8,128)(2,1)S(1)} %get-tuple-element.449), channel_id=1, source_target_pairs={{4,0},{8,4},{12,8},{5,1},{9,5},{13,9},{6,2},{10,6},{14,10},{7,3},{... | collective-permute-start | bytes 393224 | tf_op jit(solution)/shard_map/while/body/eval_jaxpr/ppermute | solution.py:12
  1443.1 0.7 copy-start.2
Sparse Core Ops, SparseCore 0:
  26.1 46.6 all-reduce.4
  150.7 52.6 all-reduce.4
  281.2 52.6 all-reduce.4
  411.7 52.6 all-reduce.4
  542.3 52.6 all-reduce.4
  672.8 52.6 all-reduce.4
  803.3 52.6 all-reduce.4
  933.8 52.6 all-reduce.4
  1064.4 52.6 all-reduce.4
  1194.9 52.6 all-reduce.4
  1325.4 52.6 all-reduce.4
where the time goes:
time: 1470 us; the launch traced here: 1450 us
  blocking collectives  694 us (47%)
  waiting for transfers between devices  567 us (39%)
  matrix products  77.6 us (5%)
  other arithmetic  51.4 us (3%)
  local copies, waits for them, and re-layouts  27.7 us (2%)
  between operations  15.8 us (1%)
    psum x11, blocking collectives, turn(): sketch = lax.psum(sketch, 'dp')  694 us
    psum x11, waiting for transfers between devices, process(): lax.psum((jnp.stack(act_parts), jnp.stack(delta_parts)), 'tensor')  567 us
    dot_general x33, matrix products, process(): jnp.dot(flat_act, dense[slot, :, :rank], preferred_element_type=jnp.float32)  35.7 us
  transfers between devices with their start and end apart: 22, of which 11 were waited for; matrix products, arithmetic and copies ran while one was open for 6% of the time, Pallas kernels for 0%

commit v1 on v0

v1 whole, which is shorter than its diff:
```python
import functools
import math

import jax
import jax.numpy as jnp
from jax import lax
from jax.experimental import pallas as pl
from jax.experimental.pallas import tpu as pltpu
from jax.sharding import PartitionSpec as P

MESH = pl.DeviceIdType.MESH
GROUPS = 2
BLOCK = 8


def silu_slope(value):
    half = jnp.tanh(0.5 * value) * 0.5
    sig = 0.5 + half
    return sig * (1.0 + value * (0.5 - half))


def kernel(
    n_dp, n_pipe, n_tensor, scale,
    sizes, blocks, grad_hbm, acts_hbm, mix_hbm, tiles_hbm,
    gout_hbm, sk_hbm,
    acts, gin, gout, mix, tiles, dense, slope, delta, parts, red, sums, rs, tile, sk,
    acts_sem, grad_sem, weight_sem, gout_sem, sk_sem,
    relay_send, relay_recv, part_send, part_recv,
    rs_send, rs_recv, dp_send, dp_recv, tn_send, tn_recv,
):
    slots, micro, tokens, width = acts.shape
    heads = mix.shape[1]
    hs = mix.shape[2]
    rank = tiles.shape[3] // 2
    rows = sums.shape[1]
    pieces = rows // BLOCK
    turns = micro // n_tensor
    dp = lax.axis_index("dp")
    pipe = lax.axis_index("pipe")
    tensor = lax.axis_index("tensor")
    top = pipe == n_pipe - 1
    live = sizes[pipe]

    def device(d, p, t):
        return {"dp": d, "pipe": p, "tensor": t}

    mix_load = pltpu.make_async_copy(mix_hbm, mix, weight_sem.at[0])
    tiles_load = pltpu.make_async_copy(tiles_hbm, tiles, weight_sem.at[1])

    def acts_load(m):
        return pltpu.make_async_copy(acts_hbm.at[:, m], acts.at[:, m], acts_sem.at[m])

    def grad_load(m):
        return pltpu.make_async_copy(grad_hbm.at[m], gin.at[m], grad_sem.at[m])

    mix_load.start()
    acts_load(0).start()

    @pl.when(top)
    def _():
        grad_load(0).start()

    tiles_load.start()

    barrier = pltpu.get_barrier_semaphore()

    def greet(d, p, t):
        pl.semaphore_signal(barrier, inc=1, device_id=device(d, p, t), device_id_type=MESH)

    @pl.when(pipe > 0)
    def _():
        greet(dp, pipe - 1, tensor)

    @pl.when(pipe < n_pipe - 1)
    def _():
        greet(dp, pipe + 1, tensor)

    def greet_tensor(o, c):
        greet(dp, pipe, lax.rem(tensor + o, n_tensor))
        return c

    def greet_dp(o, c):
        greet(lax.rem(dp + o, n_dp), pipe, tensor)
        return c

    lax.fori_loop(1, n_tensor, greet_tensor, 0)
    lax.fori_loop(1, n_dp, greet_dp, 0)

    def load_rest(m, c):
        acts_load(m).start()

        @pl.when(top)
        def _():
            grad_load(m).start()

        return c

    lax.fori_loop(1, micro, load_rest, 0)

    def slopes(m):
        acts_load(m).wait()
        for k in range(slots):
            for h in range(heads):
                cols = pl.ds(h * hs, hs)
                pre = jnp.dot(acts[k, m, :, cols], mix[k, h], preferred_element_type=jnp.float32)
                slope[k, :, cols] = silu_slope(pre)

    def relay(m, q):
        cols = pl.ds(q * (width // GROUPS), width // GROUPS)
        return pltpu.make_async_remote_copy(
            src_ref=gout.at[m, :, cols], dst_ref=gin.at[m, :, cols],
            send_sem=relay_send.at[m, q], recv_sem=relay_recv.at[m, q],
            device_id=device(dp, lax.rem(pipe + n_pipe - 1, n_pipe), tensor), device_id_type=MESH,
        )

    def part_copy(m):
        owner = lax.rem(m, n_tensor)
        turn = m // n_tensor
        source = lax.rem(tensor - owner + n_tensor + n_tensor - 1, n_tensor)
        return pltpu.make_async_remote_copy(
            src_ref=parts.at[m], dst_ref=red.at[turn, source],
            send_sem=part_send.at[m], recv_sem=part_recv.at[turn, source],
            device_id=device(dp, pipe, owner), device_id_type=MESH,
        )

    def chain(m):
        @pl.when(top)
        def _():
            grad_load(m).wait()

        for q in range(GROUPS):
            @pl.when(jnp.logical_not(top))
            def _():
                relay(m, q).wait_recv()

            for h in range(q * heads // GROUPS, (q + 1) * heads // GROUPS):
                cols = pl.ds(h * hs, hs)
                g = gin[m, :, cols].astype(jnp.float32)
                for k in range(slots - 1, -1, -1):
                    d = (g * slope[k, :, cols]).astype(jnp.bfloat16)
                    delta[k, :, cols] = d
                    back = lax.dot_general(
                        d, mix[k, h], (((1,), (1,)), ((), ())), preferred_element_type=jnp.float32
                    )
                    moved = (g + back).astype(jnp.bfloat16).astype(jnp.float32)
                    g = jnp.where(k < live, moved, g)
                gout[m, :, cols] = g.astype(jnp.bfloat16)

            @pl.when(pipe > 0)
            def _():
                relay(m, q).start()

        pltpu.make_async_copy(gout.at[m], gout_hbm.at[m], gout_sem.at[m]).start()

    lanes = lax.broadcasted_iota(jnp.int32, (tokens, 2 * rank), 1)
    low = lanes < rank

    def project(m):
        for k in range(slots):
            both = jnp.concatenate([acts[k, m], delta[k]], axis=0)
            out = jnp.dot(both, dense[k], preferred_element_type=jnp.float32)
            parts[m, k] = jnp.where(low, out[:tokens], out[tokens:]).astype(jnp.bfloat16)

        @pl.when(lax.rem(m, n_tensor) != tensor)
        def _():
            part_copy(m).start()

    mix_load.wait()
    slopes(0)

    tiles_load.wait()
    r_in = lax.broadcasted_iota(jnp.int32, (2 * rank, 2 * rank), 0)
    r_out = lax.broadcasted_iota(jnp.int32, (2 * rank, 2 * rank), 1)
    back_out = r_out - rank
    half = rank // 2
    from_row = jnp.where(
        r_out < rank, r_out,
        rank + jnp.where(back_out < half, 2 * back_out, 2 * (back_out - half) + 1),
    )
    shuffle = jnp.where(r_in == from_row, 1.0, 0.0).astype(jnp.bfloat16)
    for k in range(slots):
        for b in range(heads):
            wanted = tensor * heads + b
            pick = 0
            found = 0
            for j in range(tiles.shape[1]):
                hit = blocks[k * tiles.shape[1] + j] == wanted
                pick = jnp.where(hit, j, pick)
                found = jnp.where(hit, 1, found)
            block = jnp.dot(tiles[k, pick], shuffle, preferred_element_type=jnp.float32)
            dense[k, pl.ds(b * hs, hs), :] = jnp.where(found == 1, block, 0.0).astype(jnp.bfloat16)

    peers = (n_tensor - 1) + (n_dp - 1)

    @pl.when(jnp.logical_and(pipe > 0, pipe < n_pipe - 1))
    def _():
        pl.semaphore_wait(barrier, peers + 2)

    @pl.when(jnp.logical_or(pipe == 0, pipe == n_pipe - 1))
    def _():
        pl.semaphore_wait(barrier, peers + 1)

    def step(m, c):
        chain(m)
        project(m)

        @pl.when(m + 1 < micro)
        def _():
            slopes(m + 1)

        return c

    lax.fori_loop(0, micro, step, 0)

    def piece_of(d):
        return lax.rem(d - 4 * tensor + 4 * n_dp, n_dp)

    def rs_copy(turn, peer, r, slot):
        return pltpu.make_async_remote_copy(
            src_ref=sums.at[turn, pl.ds(r * BLOCK, BLOCK)], dst_ref=rs.at[turn, slot],
            send_sem=rs_send.at[turn, slot], recv_sem=rs_recv.at[turn, slot],
            device_id=device(peer, pipe, tensor), device_id_type=MESH,
        )

    def dp_copy(turn, m, peer, r, slot):
        return pltpu.make_async_remote_copy(
            src_ref=tile.at[turn], dst_ref=sk.at[m, pl.ds(r * BLOCK, BLOCK)],
            send_sem=dp_send.at[turn, slot], recv_sem=dp_recv.at[turn, r],
            device_id=device(peer, pipe, tensor), device_id_type=MESH,
        )

    def tensor_copy(turn, m, o):
        return pltpu.make_async_remote_copy(
            src_ref=sk.at[m], dst_ref=sk.at[m],
            send_sem=tn_send.at[turn, o - 1], recv_sem=tn_recv.at[turn, o - 1],
            device_id=device(dp, pipe, lax.rem(tensor + o, n_tensor)), device_id_type=MESH,
        )

    mine = piece_of(dp)
    packed = lax.broadcasted_iota(jnp.int32, (rank // 2, 2 * rank), 1) < rank
    for turn in range(turns):
        m = turn * n_tensor + tensor
        for s in range(n_tensor - 1):
            pltpu.make_async_copy(red.at[turn, s], red.at[turn, s], part_recv.at[turn, s]).wait()
        for k in range(slots):
            x = parts[m, k].astype(jnp.float32)
            for s in range(n_tensor - 1):
                x = x + red[turn, s, k].astype(jnp.float32)
            y = jnp.where(low, x, pltpu.roll(x, rank, 1))
            t = lax.dot_general(
                x, y, (((0,), (0,)), ((), ())), precision=lax.Precision.HIGHEST,
                preferred_element_type=jnp.float32,
            )
            out = jnp.where(packed, t[rank : rank + half], t[rank + half :]) * scale
            sums[turn, pl.ds(k * (rank // 2), rank // 2), :] = jnp.where(k < live, out, 0.0)

        def scatter(o, c):
            peer = lax.rem(dp + o, n_dp)
            r = piece_of(peer)

            @pl.when(r < pieces)
            def _():
                rs_copy(turn, peer, r, o).start()

            return c

        lax.fori_loop(1, n_dp, scatter, 0)

    for turn in range(turns):
        m = turn * n_tensor + tensor

        @pl.when(mine < pieces)
        def _():
            def arrive(o, c):
                pltpu.make_async_copy(rs.at[turn, o], rs.at[turn, o], rs_recv.at[turn, o]).wait()
                return c

            lax.fori_loop(1, n_dp, arrive, 0)
            total = sums[turn, pl.ds(mine * BLOCK, BLOCK), :]
            for o in range(1, n_dp):
                total = total + rs[turn, o]
            tile[turn] = total
            sk[m, pl.ds(mine * BLOCK, BLOCK), :] = total

            def spread(o, c):
                dp_copy(turn, m, lax.rem(dp + o, n_dp), mine, o).start()
                return c

            lax.fori_loop(1, n_dp, spread, 0)

    for turn in range(turns):
        m = turn * n_tensor + tensor

        def collect(r, c):
            @pl.when(r != mine)
            def _():
                pltpu.make_async_copy(tile.at[turn], tile.at[turn], dp_recv.at[turn, r]).wait()

            return c

        lax.fori_loop(0, pieces, collect, 0)
        for o in range(1, n_tensor):
            tensor_copy(turn, m, o).start()

    for turn in range(turns):
        for o in range(1, n_tensor):
            pltpu.make_async_copy(sk.at[0], sk.at[0], tn_recv.at[turn, o - 1]).wait()
    out_copy = pltpu.make_async_copy(sk, sk_hbm, sk_sem)
    out_copy.start()

    def drain(m, c):
        @pl.when(pipe > 0)
        def _():
            for q in range(GROUPS):
                relay(m, q).wait_send()

        @pl.when(lax.rem(m, n_tensor) != tensor)
        def _():
            part_copy(m).wait_send()

        pltpu.make_async_copy(gout.at[m], gout_hbm.at[m], gout_sem.at[m]).wait()
        return c

    lax.fori_loop(0, micro, drain, 0)
    for turn in range(turns):
        m = turn * n_tensor + tensor

        def drain_rs(o, c):
            peer = lax.rem(dp + o, n_dp)
            r = piece_of(peer)

            @pl.when(r < pieces)
            def _():
                rs_copy(turn, peer, r, o).wait_send()

            @pl.when(mine < pieces)
            def _():
                dp_copy(turn, m, peer, mine, o).wait_send()

            return c

        lax.fori_loop(1, n_dp, drain_rs, 0)
        for o in range(1, n_tensor):
            tensor_copy(turn, m, o).wait_send()
    out_copy.wait()


def shards(n_dp, n_pipe, n_tensor, grad_out, activations, mixing, proj_tiles, proj_blocks, section_sizes):
    micro, tokens, width = grad_out.shape
    slots = activations.shape[1]
    heads, hs = mixing.shape[2:4]
    n_tiles = proj_tiles.shape[2]
    rank = proj_tiles.shape[4] // 2
    rows = slots * rank // 2
    turns = micro // n_tensor
    pieces = rows // BLOCK
    bf16, f32 = jnp.bfloat16, jnp.float32
    anywhere = pl.BlockSpec(memory_space=pl.ANY)
    smem = pl.BlockSpec(memory_space=pltpu.SMEM)
    dma = pltpu.SemaphoreType.DMA
    gout, sk = pl.pallas_call(
        functools.partial(kernel, n_dp, n_pipe, n_tensor, 1.0 / math.sqrt(tokens * n_dp)),
        out_shape=(
            jax.ShapeDtypeStruct((micro, tokens, width), bf16),
            jax.ShapeDtypeStruct((micro, rows, 2 * rank), f32),
        ),
        in_specs=[smem, smem, anywhere, anywhere, anywhere, anywhere],
        out_specs=(anywhere, anywhere),
        scratch_shapes=[
            pltpu.VMEM((slots, micro, tokens, width), bf16),
            pltpu.VMEM((micro, tokens, width), bf16),
            pltpu.VMEM((micro, tokens, width), bf16),
            pltpu.VMEM((slots, heads, hs, hs), bf16),
            pltpu.VMEM((slots, n_tiles, hs, 2 * rank), bf16),
            pltpu.VMEM((slots, width, 2 * rank), bf16),
            pltpu.VMEM((slots, tokens, width), f32),
            pltpu.VMEM((slots, tokens, width), bf16),
            pltpu.VMEM((micro, slots, tokens, 2 * rank), bf16),
            pltpu.VMEM((turns, n_tensor - 1, slots, tokens, 2 * rank), bf16),
            pltpu.VMEM((turns, rows, 2 * rank), f32),
            pltpu.VMEM((turns, n_dp, BLOCK, 2 * rank), f32),
            pltpu.VMEM((turns, BLOCK, 2 * rank), f32),
            pltpu.VMEM((micro, rows, 2 * rank), f32),
            dma((micro,)), dma((micro,)), dma((2,)), dma((micro,)), dma,
            dma((micro, GROUPS)), dma((micro, GROUPS)),
            dma((micro,)), dma((turns, n_tensor - 1)),
            dma((turns, n_dp)), dma((turns, n_dp)),
            dma((turns, n_dp)), dma((turns, pieces)),
            dma((turns, n_tensor - 1)), dma((turns, n_tensor - 1)),
        ],
        compiler_params=pltpu.CompilerParams(
            collective_id=0, has_side_effects=True, vmem_limit_bytes=48 << 20
        ),
    )(
        section_sizes, proj_blocks[0].reshape(-1), grad_out, activations[0], mixing[0], proj_tiles[0],
    )
    sk = sk.reshape(micro, slots, rank // 2, 2 * rank).transpose(1, 0, 2, 3)
    return gout[None], sk.reshape(1, slots, micro, rank * rank)


def solution(mesh):
    return jax.shard_map(
        functools.partial(shards, mesh.shape["dp"], mesh.shape["pipe"], mesh.shape["tensor"]),
        mesh=mesh,
        in_specs=(
            P(None, "dp", "tensor"),
            P("pipe", None, None, "dp", "tensor"),
            P("pipe", None, "tensor", None, None),
            P("pipe", None, None, None, None),
            P("pipe", None, None),
            P(),
        ),
        out_specs=(P("pipe", None, "dp", "tensor"), P("pipe", None, None, None)),
        check_vma=False,
    )
```

time: 1470 us -> 77.6 us (0.05); the launches traced: 1450 us -> 77.4 us
  blocking collectives: 694 us -> 0 us
  waiting for transfers between devices: 567 us -> 0 us
  matrix products: 77.6 us -> 0 us
  Pallas kernels: 0 us -> 69.8 us
  other arithmetic: 51.4 us -> 0.7 us
  local copies, waits for them, and re-layouts: 27.7 us -> 6.18 us
  between operations: 15.8 us -> 0.64 us
    psum x11 -> x0, blocking collectives: 694 us -> none  [turn(): sketch = lax.psum(sketch, 'dp')]
    psum x11 -> x0, waiting for transfers between devices: 567 us -> none  [process(): lax.psum((jnp.stack(act_parts), jnp.stack(delta_parts)), 'tensor')]
    dot_general x144 -> x0, matrix products: 77.6 us -> none  [the longest x33 35.7 us: process(): jnp.dot(flat_act, dense[slot, :, :rank], preferred_element_type=jnp.float32)]
    pallas_call x0 -> x1, Pallas kernels: none -> 69.8 us  [shards(): pl.pallas_call(functools.partial(kernel, n_dp, n_pipe, n_tensor, 1.0 / ma...]
    dynamic_update_slice x11 -> x0, other arithmetic: 17.9 us -> none  [turn(): lax.dynamic_update_slice_in_dim(segment_out, jnp.where(valid, grad, old_o...]
  transfers between devices with their start and end apart: 22 -> 0, of which waited for: 11 -> 0; matrix products, arithmetic and copies ran while one was open for 6% -> 0% of each run, Pallas kernels for 0% -> 0%
where the time goes in v1:
time: 77.6 us; the launch traced here: 77.4 us
  Pallas kernels  69.8 us (90%)
  local copies, waits for them, and re-layouts  6.18 us (8%)
    pallas_call x1, Pallas kernels, shards(): pl.pallas_call(functools.partial(kernel, n_dp, n_pipe, n_tensor, 1.0 / ma...  69.8 us
    unnamed x9, local copies, waits for them, and re-layouts  5.12 us

profile of v1, /device:TPU:1, one launch (start us, length us, event | category | flops | bytes accessed | tf_op | source)
XLA Modules:
  0.0 77.4 jit_solution(12028526122869265532)
XLA Ops:
  0.6 0.7 reduce
  1.3 0.1 reshape_squeeze.3.blocks
  1.4 0.0 copy-start
  1.4 1.2 %copy-done = bf16[8,64,1024]{2,1,0:T(8,128)(2,1)S(1)} copy-done((bf16[8,64,1024]{2,1,0:T(8,128)(2,1)S(1)}, bf16[8,64,1024]{2,1,0:T(8,128)(2,1)}, u32[]{:S(2)}) %copy-start) | copy-done | bytes 1048600
  2.6 0.0 copy-start.1
  2.6 1.1 %copy-done.1 = bf16[1,3,8,128,128]{4,3,2,1,0:T(8,128)(2,1)S(1)} copy-done((bf16[1,3,8,128,128]{4,3,2,1,0:T(8,128)(2,1)S(1)}, bf16[1,3,8,128,128]{4,3,2,1,0:T(8,128)(2,1)}, u32[]{:S(2)}) %copy-start.1) | copy-done | bytes 786456
  3.8 0.0 copy-start.2
  3.8 1.1 %copy-done.2 = bf16[1,3,8,128,128]{4,3,2,1,0:T(8,128)(2,1)S(1)} copy-done((bf16[1,3,8,128,128]{4,3,2,1,0:T(8,128)(2,1)S(1)}, bf16[1,3,8,128,128]{4,3,2,1,0:T(8,128)(2,1)}, u32[]{:S(2)}) %copy-start.2) | copy-done | bytes 786456
  4.9 0.0 copy-start.3
  4.9 0.7 copy-done.3
  5.6 69.8 %shard_map.77 = (bf16[8,64,1024]{2,1,0:T(8,128)(2,1)S(1)}, f32[8,96,128]{2,1,0:T(8,128)S(1)}) custom-call(s32[4]{0:T(128)S(1)} %copy-done.3, s32[24]{0:T(128)S(1)} %reshape_squeeze.3.blocks, bf16[8,64,1024]{2,1,0:T(8,128)(2,1)S(1)} %copy-done, bf16[3,8,64,1024]{3,2,1,0:T(8,128)(2,1)} %bitcast.14, bf16[3,8,128,128]{3,2,1,0:T(8,128)(2,1)S(1)} %bitcast.11, ...), custom_call_target="tpu_custom_call" | custom-call | tf_op jit(solution)/shard_map/pallas_call | solution.py:361
  75.4 1.0 %copy.10 = f32[3,8,32,128]{3,1,2,0:T(8,128)} copy(f32[3,8,32,128]{3,2,0,1:T(8,128)S(1)} %bitcast.13) | data formatting | bytes 786432 | tf_op jit(solution)/shard_map/transpose | solution.py:397
  76.4 1.0 %copy.12 = bf16[1,8,64,1024]{3,2,1,0:T(8,128)(2,1)} copy(bf16[1,8,64,1024]{3,2,1,0:T(8,128)(2,1)S(1)} %bitcast.10) | data formatting | bytes 2097152
Async XLA Ops:
  1.4 1.2 %copy-start = (bf16[8,64,1024]{2,1,0:T(8,128)(2,1)S(1)}, bf16[8,64,1024]{2,1,0:T(8,128)(2,1)}, u32[]{:S(2)}) copy-start(bf16[8,64,1024]{2,1,0:T(8,128)(2,1)} %grad_hbm.1) | copy-start | bytes 3145732
  2.6 1.1 %copy-start.1 = (bf16[1,3,8,128,128]{4,3,2,1,0:T(8,128)(2,1)S(1)}, bf16[1,3,8,128,128]{4,3,2,1,0:T(8,128)(2,1)}, u32[]{:S(2)}) copy-start(bf16[1,3,8,128,128]{4,3,2,1,0:T(8,128)(2,1)} %param.8) | copy-start | bytes 2359300
  3.8 1.1 %copy-start.2 = (bf16[1,3,8,128,128]{4,3,2,1,0:T(8,128)(2,1)S(1)}, bf16[1,3,8,128,128]{4,3,2,1,0:T(8,128)(2,1)}, u32[]{:S(2)}) copy-start(bf16[1,3,8,128,128]{4,3,2,1,0:T(8,128)(2,1)} %param.9) | copy-start | bytes 2359300
  4.9 0.7 copy-start.3

commit v2 on v1

v2 whole, which is shorter than its diff:
```python
import functools
import math

import jax
import jax.numpy as jnp
from jax import lax
from jax.experimental import pallas as pl
from jax.experimental.pallas import tpu as pltpu
from jax.sharding import PartitionSpec as P

MESH = pl.DeviceIdType.MESH
GROUPS = 2


def silu_slope(value):
    half = jnp.tanh(0.5 * value) * 0.5
    sig = 0.5 + half
    return sig * (1.0 + value * (0.5 - half))


def kernel(
    n_dp, n_pipe, n_tensor, scale,
    sizes, blocks, grad_hbm, acts_hbm, mix_hbm, tiles_hbm,
    gout, sk_out,
    acts, gin, mix, tiles, dense, slope, delta, parts, red, zbuf, sk, wide,
    acts_sem, grad_sem, weight_sem,
    relay_send, relay_recv, part_send, part_recv, z_send, z_recv, x_send, x_recv,
):
    slots, micro, tokens, width = acts.shape
    heads = mix.shape[1]
    hs = mix.shape[2]
    n_tiles = tiles.shape[1]
    rank = tiles.shape[3] // 2
    half = rank // 2
    ring = 2 * n_tensor
    n_z = n_dp // 2
    rounds = zbuf.shape[0]
    dp = lax.axis_index("dp")
    pipe = lax.axis_index("pipe")
    tensor = lax.axis_index("tensor")
    z = dp // 2
    side = lax.rem(dp, 2)
    me = side * n_tensor + tensor
    top = pipe == n_pipe - 1
    live = sizes[pipe]

    def at(zz, u, p=None):
        return {
            "dp": zz * 2 + u // n_tensor,
            "pipe": pipe if p is None else p,
            "tensor": lax.rem(u, n_tensor),
        }

    mix_load = pltpu.make_async_copy(mix_hbm.at[0], mix, weight_sem.at[0])
    tiles_load = pltpu.make_async_copy(tiles_hbm.at[0], tiles, weight_sem.at[1])

    def acts_load(m):
        return pltpu.make_async_copy(acts_hbm.at[0, :, m], acts.at[:, m], acts_sem.at[m])

    def grad_load(m):
        return pltpu.make_async_copy(grad_hbm.at[m], gin.at[m], grad_sem.at[m])

    mix_load.start()
    acts_load(0).start()

    @pl.when(top)
    def _():
        grad_load(0).start()

    barrier = pltpu.get_barrier_semaphore()

    def greet(where):
        pl.semaphore_signal(barrier, inc=1, device_id=where, device_id_type=MESH)

    @pl.when(pipe < n_pipe - 1)
    def _():
        greet(at(z, me, pipe + 1))

    @pl.when(pipe > 0)
    def _():
        greet(at(z, me, pipe - 1))

    for o in range(1, n_z):
        greet(at(lax.rem(z + o, n_z), me))
    for o in range(1, ring):
        greet(at(z, lax.rem(me + o, ring)))
    tiles_load.start()

    def load_rest(m, c):
        acts_load(m).start()

        @pl.when(top)
        def _():
            grad_load(m).start()

        return c

    lax.fori_loop(1, micro, load_rest, 0)

    def slopes(m):
        acts_load(m).wait()
        for h in range(heads):
            cols = pl.ds(h * hs, hs)
            for k in range(slots):
                pre = jnp.dot(acts[k, m, :, cols], mix[k, h], preferred_element_type=jnp.float32)
                slope[k, :, cols] = silu_slope(pre)

    def relay(m, q):
        cols = pl.ds(q * (width // GROUPS), width // GROUPS)
        return pltpu.make_async_remote_copy(
            src_ref=gout.at[m, :, cols], dst_ref=gin.at[m, :, cols],
            send_sem=relay_send.at[m, q], recv_sem=relay_recv.at[m, q],
            device_id=at(z, me, lax.rem(pipe + n_pipe - 1, n_pipe)), device_id_type=MESH,
        )

    def part_copy(m, k):
        n = m * slots + k
        owner = lax.rem(n, ring)
        turn = n // ring
        gap = lax.rem(tensor - lax.rem(owner, n_tensor) + n_tensor, n_tensor)
        slot = jnp.where(owner // n_tensor == side, gap - 1, n_tensor - 1 + gap)
        slot = jnp.maximum(slot, 0)
        return owner, pltpu.make_async_remote_copy(
            src_ref=parts.at[n], dst_ref=red.at[turn, slot],
            send_sem=part_send.at[n], recv_sem=part_recv.at[turn, slot],
            device_id=at(z, owner), device_id_type=MESH,
        )

    def chain(m):
        @pl.when(top)
        def _():
            grad_load(m).wait()

        for q in range(GROUPS):
            @pl.when(jnp.logical_not(top))
            def _():
                relay(m, q).wait_recv()

            for h in range(q * heads // GROUPS, (q + 1) * heads // GROUPS):
                cols = pl.ds(h * hs, hs)
                g = gin[m, :, cols].astype(jnp.float32)
                for k in range(slots - 1, -1, -1):
                    d = (g * slope[k, :, cols]).astype(jnp.bfloat16)
                    delta[k, :, cols] = d
                    back = lax.dot_general(
                        d, mix[k, h], (((1,), (1,)), ((), ())), preferred_element_type=jnp.float32
                    )
                    moved = (g + back).astype(jnp.bfloat16).astype(jnp.float32)
                    g = jnp.where(k < live, moved, g)
                gout[m, :, cols] = g.astype(jnp.bfloat16)

            @pl.when(pipe > 0)
            def _():
                relay(m, q).start()

    def low(size):
        return lax.broadcasted_iota(jnp.int32, (size, 2 * rank), 1) < rank

    def project(m):
        for k in range(slots - 1, -1, -1):
            both = jnp.concatenate([acts[k, m], delta[k]], axis=0)
            out = jnp.dot(both, dense[k], preferred_element_type=jnp.float32)
            parts[m * slots + k] = jnp.where(
                low(tokens), out[:tokens], out[tokens:]
            ).astype(jnp.bfloat16)
            owner, copy = part_copy(m, k)

            @pl.when(owner != me)
            def _():
                copy.start()

    def build():
        tiles_load.wait()
        r_in = lax.broadcasted_iota(jnp.int32, (2 * rank, 2 * rank), 0)
        r_out = lax.broadcasted_iota(jnp.int32, (2 * rank, 2 * rank), 1)
        moved = r_out - rank
        from_row = jnp.where(
            r_out < rank, r_out,
            rank + jnp.where(moved < half, 2 * moved, 2 * (moved - half) + 1),
        )
        shuffle = jnp.where(r_in == from_row, 1.0, 0.0).astype(jnp.bfloat16)
        for k in range(slots):
            for b in range(heads):
                wanted = tensor * heads + b
                pick = 0
                found = 0
                for j in range(n_tiles):
                    hit = blocks[k, 0, j] == wanted
                    pick = jnp.where(hit, j, pick)
                    found = jnp.where(hit, 1, found)
                block = jnp.dot(tiles[k, pick], shuffle, preferred_element_type=jnp.float32)
                dense[k, pl.ds(b * hs, hs), :] = jnp.where(found == 1, block, 0.0).astype(jnp.bfloat16)

    def z_copy(r, o):
        return pltpu.make_async_remote_copy(
            src_ref=zbuf.at[r, z], dst_ref=zbuf.at[r, z],
            send_sem=z_send.at[r, o - 1], recv_sem=z_recv.at[r, o - 1],
            device_id=at(lax.rem(z + o, n_z), me), device_id_type=MESH,
        )

    def x_copy(r, o):
        n = r * ring + me
        return pltpu.make_async_remote_copy(
            src_ref=sk.at[n], dst_ref=sk.at[n],
            send_sem=x_send.at[r, o - 1], recv_sem=x_recv.at[r, o - 1],
            device_id=at(z, lax.rem(me + o, ring)), device_id_type=MESH,
        )

    def outer(r):
        n = r * ring + me
        for s in range(ring - 1):
            pltpu.make_async_copy(red.at[r, s], red.at[r, s], part_recv.at[r, s]).wait()
        near = parts[n].astype(jnp.float32)
        for s in range(n_tensor - 1):
            near = near + red[r, s].astype(jnp.float32)
        far = red[r, n_tensor - 1].astype(jnp.float32)
        for s in range(n_tensor, ring - 1):
            far = far + red[r, s].astype(jnp.float32)
        x = jnp.concatenate([near, far], axis=0)
        y = jnp.where(low(2 * tokens), x, pltpu.roll(x, rank, 1))
        t = lax.dot_general(
            x, y, (((0,), (0,)), ((), ())), precision=lax.Precision.HIGHEST,
            preferred_element_type=jnp.float32,
        )
        out = jnp.where(low(half), t[rank : rank + half], t[rank + half :]) * scale
        zbuf[r, z] = jnp.where(lax.rem(n, slots) < live, out, 0.0).astype(jnp.bfloat16)
        for o in range(1, n_z):
            z_copy(r, o).start()

    def finish(r):
        for o in range(1, n_z):
            z_copy(r, o).wait_recv()
        total = zbuf[r, 0].astype(jnp.float32)
        for zz in range(1, n_z):
            total = total + zbuf[r, zz].astype(jnp.float32)
        sk[r * ring + me] = total.astype(jnp.bfloat16)
        for o in range(1, ring):
            x_copy(r, o).start()

    mix_load.wait()
    slopes(0)
    greeted = (n_z - 1) + (ring - 1)

    @pl.when(jnp.logical_and(pipe > 0, pipe < n_pipe - 1))
    def _():
        pl.semaphore_wait(barrier, greeted + 2)

    @pl.when(jnp.logical_or(pipe == 0, pipe == n_pipe - 1))
    def _():
        pl.semaphore_wait(barrier, greeted + 1)

    def step(m, c):
        chain(m)

        @pl.when(m == 0)
        def _():
            build()

        project(m)

        @pl.when(m + 1 < micro)
        def _():
            slopes(m + 1)

        for r in range(rounds - 1):
            @pl.when(m == (ring * (r + 1) - 1) // slots + 2)
            def _():
                outer(r)

        for r in range(rounds - 2):
            @pl.when(m == (ring * (r + 1) - 1) // slots + 4)
            def _():
                finish(r)

        return c

    lax.fori_loop(0, micro, step, 0)
    outer(rounds - 1)
    finish(rounds - 2)
    finish(rounds - 1)

    for r in range(rounds):
        for o in range(1, ring):
            x_copy(r, o).wait_recv()
    for n in range(slots * micro):
        wide[pl.ds(n * half, half), :] = sk[n].astype(jnp.float32)
    for k in range(slots):
        for i in range(half):
            sk_out[0, k, :, pl.ds(i * 2 * rank, 2 * rank)] = wide[
                pl.ds(k * half + i, micro, stride=slots * half), :
            ]

    def drain(m, c):
        @pl.when(pipe > 0)
        def _():
            for q in range(GROUPS):
                relay(m, q).wait_send()

        for k in range(slots):
            owner, copy = part_copy(m, k)

            @pl.when(owner != me)
            def _():
                copy.wait_send()

        return c

    lax.fori_loop(0, micro, drain, 0)
    for r in range(rounds):
        for o in range(1, n_z):
            z_copy(r, o).wait_send()
        for o in range(1, ring):
            x_copy(r, o).wait_send()


def shards(n_dp, n_pipe, n_tensor, grad_out, activations, mixing, proj_tiles, proj_blocks, section_sizes):
    micro, tokens, width = grad_out.shape
    slots = activations.shape[1]
    heads, hs = mixing.shape[2:4]
    n_tiles = proj_tiles.shape[2]
    rank = proj_tiles.shape[4] // 2
    units = micro * slots
    ring = 2 * n_tensor
    rounds = units // ring
    n_z = n_dp // 2
    bf16, f32 = jnp.bfloat16, jnp.float32
    hbm = pl.BlockSpec(memory_space=pltpu.HBM)
    vmem = pl.BlockSpec(memory_space=pltpu.VMEM)
    smem = pl.BlockSpec(memory_space=pltpu.SMEM)
    dma = pltpu.SemaphoreType.DMA
    gout, sk = pl.pallas_call(
        functools.partial(kernel, n_dp, n_pipe, n_tensor, 1.0 / math.sqrt(tokens * n_dp)),
        out_shape=(
            jax.ShapeDtypeStruct((micro, tokens, width), bf16),
            jax.ShapeDtypeStruct((1, slots, micro, rank * rank), f32),
        ),
        in_specs=[smem, smem, hbm, hbm, hbm, hbm],
        out_specs=(vmem, vmem),
        scratch_shapes=[
            pltpu.VMEM((slots, micro, tokens, width), bf16),
            pltpu.VMEM((micro, tokens, width), bf16),
            pltpu.VMEM((slots, heads, hs, hs), bf16),
            pltpu.VMEM((slots, n_tiles, hs, 2 * rank), bf16),
            pltpu.VMEM((slots, width, 2 * rank), bf16),
            pltpu.VMEM((slots, tokens, width), f32),
            pltpu.VMEM((slots, tokens, width), bf16),
            pltpu.VMEM((units, tokens, 2 * rank), bf16),
            pltpu.VMEM((rounds, ring - 1, tokens, 2 * rank), bf16),
            pltpu.VMEM((rounds, n_z, rank // 2, 2 * rank), bf16),
            pltpu.VMEM((units, rank // 2, 2 * rank), bf16),
            pltpu.VMEM((units * rank // 2, 2 * rank), f32),
            dma((micro,)), dma((micro,)), dma((2,)),
            dma((micro, GROUPS)), dma((micro, GROUPS)),
            dma((units,)), dma((rounds, ring - 1)),
            dma((rounds, n_z - 1)), dma((rounds, n_z - 1)),
            dma((rounds, ring - 1)), dma((rounds, ring - 1)),
        ],
        compiler_params=pltpu.CompilerParams(
            collective_id=0, has_side_effects=True, vmem_limit_bytes=67_043_328
        ),
    )(section_sizes, proj_blocks.transpose(1, 0, 2), grad_out, activations, mixing, proj_tiles)
    return gout[None], sk


def solution(mesh):
    return jax.shard_map(
        functools.partial(shards, mesh.shape["dp"], mesh.shape["pipe"], mesh.shape["tensor"]),
        mesh=mesh,
        in_specs=(
            P(None, "dp", "tensor"),
            P("pipe", None, None, "dp", "tensor"),
            P("pipe", None, "tensor", None, None),
            P("pipe", None, None, None, None),
            P("pipe", None, None),
            P(),
        ),
        out_specs=(P("pipe", None, "dp", "tensor"), P("pipe", None, None, None)),
        check_vma=False,
    )
```

time: 77.6 us -> 67.5 us (0.87)
  Pallas kernels: 69.8 us -> 62.6 us
  local copies, waits for them, and re-layouts: 6.18 us -> 4.03 us
    pallas_call x1, Pallas kernels: 69.8 us -> 62.6 us  [shards(): pl.pallas_call(functools.partial(kernel, n_dp, n_pipe, n_tensor, 1.0 / ma...]
    unnamed x9 -> x2, local copies, waits for them, and re-layouts: 5.12 us -> 4.03 us
    transpose x1 -> x0, local copies, waits for them, and re-layouts: 0.98 us -> none  [shards(): sk = sk.reshape(micro, slots, rank // 2, 2 * rank).transpose(1, 0, 2, 3)]
where the time goes in v2:
time: 67.5 us; the launch traced here: 67.3 us
  Pallas kernels  62.6 us (93%)
  local copies, waits for them, and re-layouts  4.03 us (6%)
    pallas_call x1, Pallas kernels, shards(): pl.pallas_call(functools.partial(kernel, n_dp, n_pipe, n_tensor, 1.0 / ma...  62.6 us
    unnamed x2, local copies, waits for them, and re-layouts  4.03 us

profile of v2, /device:TPU:1, one launch (start us, length us, event | category | flops | bytes accessed | tf_op | source)
XLA Modules:
  0.0 67.3 jit_solution(17612236875607205908)
XLA Ops:
  0.6 62.6 %shard_map.77 = (bf16[8,64,1024]{2,1,0:T(8,128)(2,1)}, f32[1,3,8,4096]{3,2,1,0:T(8,128)}) custom-call(s32[4]{0:T(128)} %sizes.1, s32[3,1,8]{2,1,0:T(1,128)} %bitcast.3, bf16[8,64,1024]{2,1,0:T(8,128)(2,1)} %grad_hbm.1, bf16[1,3,8,64,1024]{4,3,2,1,0:T(8,128)(2,1)} %acts_hbm.1, bf16[1,3,8,128,128]{4,3,2,1,0:T(8,128)(2,1)} %mix_hbm.1, ...), custom_call_target="tpu_custom_call" | custom-call | tf_op jit(solution)/shard_map/pallas_call | solution.py:331
  63.3 2.3 %copy.10 = bf16[1,8,64,1024]{3,2,1,0:T(8,128)(2,1)} copy(bf16[1,8,64,1024]{3,2,1,0:T(8,128)(2,1)} %bitcast.2) | data formatting | bytes 2097152
  65.5 1.8 %copy.11 = f32[1,3,8,4096]{3,2,1,0:T(8,128)} copy(f32[1,3,8,4096]{3,2,1,0:T(8,128)} %get-tuple-element.9) | data formatting | bytes 786432

commit v3 on v2

--- a/solution.py
+++ b/solution.py
@@ -16,6 +16,17 @@
     half = jnp.tanh(0.5 * value) * 0.5
     sig = 0.5 + half
     return sig * (1.0 + value * (0.5 - half))
+
+
+def store(gout, sk, gout_hbm, sk_hbm, sem):
+    copies = [
+        pltpu.make_async_copy(gout, gout_hbm.at[0], sem.at[0]),
+        pltpu.make_async_copy(sk, sk_hbm, sem.at[1]),
+    ]
+    for copy in copies:
+        copy.start()
+    for copy in copies:
+        copy.wait()
 
 
 def kernel(
@@ -97,13 +108,10 @@
 
     lax.fori_loop(1, micro, load_rest, 0)
 
-    def slopes(m):
-        acts_load(m).wait()
-        for h in range(heads):
-            cols = pl.ds(h * hs, hs)
-            for k in range(slots):
-                pre = jnp.dot(acts[k, m, :, cols], mix[k, h], preferred_element_type=jnp.float32)
-                slope[k, :, cols] = silu_slope(pre)
+    def slopes(m, k, h):
+        cols = pl.ds(h * hs, hs)
+        pre = jnp.dot(acts[k, m, :, cols], mix[k, h], preferred_element_type=jnp.float32)
+        slope[k, :, cols] = silu_slope(pre)
 
     def relay(m, q):
         cols = pl.ds(q * (width // GROUPS), width // GROUPS)
@@ -127,27 +135,39 @@
         )
 
     def chain(m):
+        after = jnp.minimum(m + 1, micro - 1)
+
         @pl.when(top)
         def _():
             grad_load(m).wait()
 
+        @pl.when(m + 1 < micro)
+        def _():
+            acts_load(after).wait()
+
         for q in range(GROUPS):
             @pl.when(jnp.logical_not(top))
             def _():
                 relay(m, q).wait_recv()
 
-            for h in range(q * heads // GROUPS, (q + 1) * heads // GROUPS):
-                cols = pl.ds(h * hs, hs)
-                g = gin[m, :, cols].astype(jnp.float32)
-                for k in range(slots - 1, -1, -1):
-                    d = (g * slope[k, :, cols]).astype(jnp.bfloat16)
+            some = range(q * heads // GROUPS, (q + 1) * heads // GROUPS)
+            g = {h: gin[m, :, pl.ds(h * hs, hs)] for h in some}
+            for k in range(slots - 1, -1, -1):
+                back = {}
+                for h in some:
+                    cols = pl.ds(h * hs, hs)
+                    d = (g[h].astype(jnp.float32) * slope[k, :, cols]).astype(jnp.bfloat16)
                     delta[k, :, cols] = d
-                    back = lax.dot_general(
+                    back[h] = lax.dot_general(
                         d, mix[k, h], (((1,), (1,)), ((), ())), preferred_element_type=jnp.float32
                     )
-                    moved = (g + back).astype(jnp.bfloat16).astype(jnp.float32)
-                    g = jnp.where(k < live, moved, g)
-                gout[m, :, cols] = g.astype(jnp.bfloat16)
+                for h in some:
+                    slopes(after, k, h)
+                for h in some:
+                    moved = (g[h].astype(jnp.float32) + back[h]).astype(jnp.bfloat16)
+                    g[h] = jnp.where(k < live, moved, g[h])
+            for h in some:
+                gout[m, :, pl.ds(h * hs, hs)] = g[h]
 
             @pl.when(pipe > 0)
             def _():
@@ -238,7 +258,10 @@
             x_copy(r, o).start()
 
     mix_load.wait()
-    slopes(0)
+    acts_load(0).wait()
+    for h in range(heads):
+        for k in range(slots):
+            slopes(0, k, h)
     greeted = (n_z - 1) + (ring - 1)
 
     @pl.when(jnp.logical_and(pipe > 0, pipe < n_pipe - 1))
@@ -257,10 +280,6 @@
             build()
 
         project(m)
-
-        @pl.when(m + 1 < micro)
-        def _():
-            slopes(m + 1)
 
         for r in range(rounds - 1):
             @pl.when(m == (ring * (r + 1) - 1) // slots + 2)
@@ -331,8 +350,8 @@
     gout, sk = pl.pallas_call(
         functools.partial(kernel, n_dp, n_pipe, n_tensor, 1.0 / math.sqrt(tokens * n_dp)),
         out_shape=(
-            jax.ShapeDtypeStruct((micro, tokens, width), bf16),
-            jax.ShapeDtypeStruct((1, slots, micro, rank * rank), f32),
+            pltpu.VMEM((micro, tokens, width), bf16),
+            pltpu.VMEM((1, slots, micro, rank * rank), f32),
         ),
         in_specs=[smem, smem, hbm, hbm, hbm, hbm],
         out_specs=(vmem, vmem),
@@ -356,10 +375,22 @@
             dma((rounds, ring - 1)), dma((rounds, ring - 1)),
         ],
         compiler_params=pltpu.CompilerParams(
-            collective_id=0, has_side_effects=True, vmem_limit_bytes=67_043_328
+            collective_id=0, has_side_effects=True, vmem_limit_bytes=40 << 20
         ),
-    )(section_sizes, proj_blocks.transpose(1, 0, 2), grad_out, activations, mixing, proj_tiles)
-    return gout[None], sk
+    )(*[
+        pltpu.with_memory_space_constraint(x, pltpu.HBM)
+        for x in (section_sizes, proj_blocks.transpose(1, 0, 2), grad_out, activations, mixing, proj_tiles)
+    ])
+    return pl.pallas_call(
+        store,
+        out_shape=(
+            jax.ShapeDtypeStruct((1,) + gout.shape, bf16), jax.ShapeDtypeStruct(sk.shape, f32),
+        ),
+        in_specs=[vmem, vmem],
+        out_specs=(hbm, hbm),
+        scratch_shapes=[dma((2,))],
+        compiler_params=pltpu.CompilerParams(vmem_limit_bytes=1 << 20),
+    )(*[pltpu.with_memory_space_constraint(x, pltpu.VMEM) for x in (gout, sk)])
 
 
 def solution(mesh):

time: 67.5 us -> 61.7 us (0.914)
  local copies, waits for them, and re-layouts: 4.03 us -> 0 us
  Pallas kernels: 62.6 us -> 61 us
    unnamed x2 -> x0, local copies, waits for them, and re-layouts: 4.03 us -> none
    pallas_call x1, Pallas kernels: 62.6 us -> 59.8 us  [shards(): pl.pallas_call(functools.partial(kernel, n_dp, n_pipe, n_tensor, 1.0 / ma...]
    pallas_call x0 -> x1, Pallas kernels: none -> 1.11 us  [shards(): pl.pallas_call(store, out_shape=(jax.ShapeDtypeStruct((1,) + gout.shape,...]
where the time goes in v3:
time: 61.7 us; the launch traced here: 61.6 us
  Pallas kernels  61 us (99%)
  between operations  0.64 us (1%)
    pallas_call x1, Pallas kernels, shards(): pl.pallas_call(functools.partial(kernel, n_dp, n_pipe, n_tensor, 1.0 / ma...  59.8 us

profile of v3, /device:TPU:1, one launch (start us, length us, event | category | flops | bytes accessed | tf_op | source)
XLA Modules:
  0.0 61.6 jit_solution(1281263703837439851)
XLA Ops:
  0.6 59.8 %shard_map.77 = (bf16[8,64,1024]{2,1,0:T(8,128)(2,1)S(1)}, f32[1,3,8,4096]{3,2,1,0:T(8,128)S(1)}) custom-call(s32[4]{0:T(128)} %sizes.1, s32[3,1,8]{2,1,0:T(1,128)} %bitcast.1, bf16[8,64,1024]{2,1,0:T(8,128)(2,1)} %grad_hbm.1, bf16[1,3,8,64,1024]{4,3,2,1,0:T(8,128)(2,1)} %acts_hbm.1, bf16[1,3,8,128,128]{4,3,2,1,0:T(8,128)(2,1)} %mix_hbm.1, ...), custom_call_target="tpu_custom_call" | custom-call | tf_op jit(solution)/shard_map/pallas_call | solution.py:350
  60.5 1.1 %shard_map.78 = (bf16[1,8,64,1024]{3,2,1,0:T(8,128)(2,1)}, f32[1,3,8,4096]{3,2,1,0:T(8,128)}) custom-call(bf16[8,64,1024]{2,1,0:T(8,128)(2,1)S(1)} %get-tuple-element.4.gout, f32[1,3,8,4096]{3,2,1,0:T(8,128)S(1)} %get-tuple-element.5.sk), custom_call_target="tpu_custom_call" | custom-call | tf_op jit(solution)/shard_map/pallas_call | solution.py:384

commit v4 on v3

--- a/solution.py
+++ b/solution.py
@@ -31,10 +31,10 @@
 
 def kernel(
     n_dp, n_pipe, n_tensor, scale,
-    sizes, blocks, grad_hbm, acts_hbm, mix_hbm, tiles_hbm,
+    sizes_hbm, blocks_hbm, grad_hbm, acts_hbm, mix_hbm, tiles_hbm,
     gout, sk_out,
-    acts, gin, mix, tiles, dense, slope, delta, parts, red, zbuf, sk, wide,
-    acts_sem, grad_sem, weight_sem,
+    sizes, blocks, acts, gin, mix, tiles, dense, slope, delta, gathered, parts, red, zbuf, sk, wide,
+    acts_sem, grad_sem, weight_sem, near_z, near_x,
     relay_send, relay_recv, part_send, part_recv, z_send, z_recv, x_send, x_recv,
 ):
     slots, micro, tokens, width = acts.shape
@@ -53,7 +53,6 @@
     side = lax.rem(dp, 2)
     me = side * n_tensor + tensor
     top = pipe == n_pipe - 1
-    live = sizes[pipe]
 
     def at(zz, u, p=None):
         return {
@@ -71,6 +70,8 @@
     def grad_load(m):
         return pltpu.make_async_copy(grad_hbm.at[m], gin.at[m], grad_sem.at[m])
 
+    sizes_load = pltpu.make_async_copy(sizes_hbm, sizes, weight_sem.at[2])
+    blocks_load = pltpu.make_async_copy(blocks_hbm, blocks, weight_sem.at[3])
     mix_load.start()
     acts_load(0).start()
 
@@ -91,11 +92,23 @@
     def _():
         greet(at(z, me, pipe - 1))
 
-    for o in range(1, n_z):
-        greet(at(lax.rem(z + o, n_z), me))
-    for o in range(1, ring):
-        greet(at(z, lax.rem(me + o, ring)))
+    beside_z = [at(lax.rem(z + o, n_z), me) for o in (1, n_z - 1)]
+    beside_x = [at(z, lax.rem(me + o, ring)) for o in (1, ring - 1)]
+    for where in beside_z + beside_x:
+        greet(where)
+    sizes_load.start()
+    blocks_load.start()
     tiles_load.start()
+
+    def tell(i):
+        for where in beside_z:
+            pl.semaphore_signal(near_z.at[i], inc=1, device_id=where, device_id_type=MESH)
+        for where in beside_x:
+            pl.semaphore_signal(near_x.at[i], inc=1, device_id=where, device_id_type=MESH)
+
+    def hear(i):
+        pl.semaphore_wait(near_z.at[i], 2)
+        pl.semaphore_wait(near_x.at[i], 2)
 
     def load_rest(m, c):
         acts_load(m).start()
@@ -134,63 +147,57 @@
             device_id=at(z, owner), device_id_type=MESH,
         )
 
-    def chain(m):
-        after = jnp.minimum(m + 1, micro - 1)
-
-        @pl.when(top)
-        def _():
-            grad_load(m).wait()
-
-        @pl.when(m + 1 < micro)
-        def _():
-            acts_load(after).wait()
-
-        for q in range(GROUPS):
-            @pl.when(jnp.logical_not(top))
-            def _():
-                relay(m, q).wait_recv()
-
-            some = range(q * heads // GROUPS, (q + 1) * heads // GROUPS)
-            g = {h: gin[m, :, pl.ds(h * hs, hs)] for h in some}
-            for k in range(slots - 1, -1, -1):
-                back = {}
-                for h in some:
-                    cols = pl.ds(h * hs, hs)
-                    d = (g[h].astype(jnp.float32) * slope[k, :, cols]).astype(jnp.bfloat16)
-                    delta[k, :, cols] = d
-                    back[h] = lax.dot_general(
-                        d, mix[k, h], (((1,), (1,)), ((), ())), preferred_element_type=jnp.float32
-                    )
-                for h in some:
-                    slopes(after, k, h)
-                for h in some:
-                    moved = (g[h].astype(jnp.float32) + back[h]).astype(jnp.bfloat16)
-                    g[h] = jnp.where(k < live, moved, g[h])
-            for h in some:
-                gout[m, :, pl.ds(h * hs, hs)] = g[h]
-
-            @pl.when(pipe > 0)
-            def _():
-                relay(m, q).start()
-
     def low(size):
         return lax.broadcasted_iota(jnp.int32, (size, 2 * rank), 1) < rank
 
-    def project(m):
+    def group(q):
+        return range(q * heads // GROUPS, (q + 1) * heads // GROUPS)
+
+    def project(m, q, k):
+        cols = pl.ds(q * (width // GROUPS), width // GROUPS)
+        both = jnp.concatenate([acts[k, m, :, cols], delta[k, :, cols]], axis=0)
+        out = jnp.dot(both, dense[k, cols], preferred_element_type=jnp.float32)
+        part = jnp.where(low(tokens), out[:tokens], out[tokens:])
+        if q > 0:
+            part = part + gathered[k]
+        if q < GROUPS - 1:
+            gathered[k] = part
+        else:
+            parts[m * slots + k] = part.astype(jnp.bfloat16)
+
+    def send_parts(m):
         for k in range(slots - 1, -1, -1):
-            both = jnp.concatenate([acts[k, m], delta[k]], axis=0)
-            out = jnp.dot(both, dense[k], preferred_element_type=jnp.float32)
-            parts[m * slots + k] = jnp.where(
-                low(tokens), out[:tokens], out[tokens:]
-            ).astype(jnp.bfloat16)
             owner, copy = part_copy(m, k)
 
             @pl.when(owner != me)
             def _():
                 copy.start()
 
-    def build():
-        tiles_load.wait()
+    def chain(m, q, after):
+        some = group(q)
+        g = {h: gin[m, :, pl.ds(h * hs, hs)] for h in some}
+        for k in range(slots - 1, -1, -1):
+            back = {}
+            for h in some:
+                cols = pl.ds(h * hs, hs)
+                d = (g[h].astype(jnp.float32) * slope[k, :, cols]).astype(jnp.bfloat16)
+                delta[k, :, cols] = d
+                back[h] = lax.dot_general(
+                    d, mix[k, h], (((1,), (1,)), ((), ())), preferred_element_type=jnp.float32
+                )
+            for h in some:
+                slopes(after, k, h)
+            if q > 0:
+                project(m, q - 1, k)
+            else:
+                project(jnp.maximum(m - 1, 0), GROUPS - 1, k)
+            for h in some:
+                moved = (g[h].astype(jnp.float32) + back[h]).astype(jnp.bfloat16)
+                g[h] = jnp.where(k < sizes[pipe], moved, g[h])
+        for h in some:
+            gout[m, :, pl.ds(h * hs, hs)] = g[h]
+
+    def build(q):
         r_in = lax.broadcasted_iota(jnp.int32, (2 * rank, 2 * rank), 0)
         r_out = lax.broadcasted_iota(jnp.int32, (2 * rank, 2 * rank), 1)
         moved = r_out - rank
@@ -200,7 +207,7 @@
         )
         shuffle = jnp.where(r_in == from_row, 1.0, 0.0).astype(jnp.bfloat16)
         for k in range(slots):
-            for b in range(heads):
+            for b in group(q):
                 wanted = tensor * heads + b
                 pick = 0
                 found = 0
@@ -243,7 +250,7 @@
             preferred_element_type=jnp.float32,
         )
         out = jnp.where(low(half), t[rank : rank + half], t[rank + half :]) * scale
-        zbuf[r, z] = jnp.where(lax.rem(n, slots) < live, out, 0.0).astype(jnp.bfloat16)
+        zbuf[r, z] = jnp.where(lax.rem(n, slots) < sizes[pipe], out, 0.0).astype(jnp.bfloat16)
         for o in range(1, n_z):
             z_copy(r, o).start()
 
@@ -259,27 +266,83 @@
 
     mix_load.wait()
     acts_load(0).wait()
-    for h in range(heads):
-        for k in range(slots):
-            slopes(0, k, h)
-    greeted = (n_z - 1) + (ring - 1)
+
+    def start_slopes(q):
+        for h in group(q):
+            for k in range(slots):
+                slopes(0, k, h)
+
+    start_slopes(0)
+    sizes_load.wait()
 
     @pl.when(jnp.logical_and(pipe > 0, pipe < n_pipe - 1))
     def _():
-        pl.semaphore_wait(barrier, greeted + 2)
+        pl.semaphore_wait(barrier, 6)
 
     @pl.when(jnp.logical_or(pipe == 0, pipe == n_pipe - 1))
     def _():
-        pl.semaphore_wait(barrier, greeted + 1)
+        pl.semaphore_wait(barrier, 5)
+
+    tell(0)
+
+    @pl.when(jnp.logical_not(top))
+    def _():
+        tiles_load.wait()
+        blocks_load.wait()
+        for q in range(GROUPS):
+            build(q)
+        hear(0)
+        tell(1)
+        for q in range(1, GROUPS):
+            start_slopes(q)
+        hear(1)
+        tell(2)
 
     def step(m, c):
-        chain(m)
-
-        @pl.when(m == 0)
+        after = jnp.minimum(m + 1, micro - 1)
+
+        @pl.when(top)
         def _():
-            build()
-
-        project(m)
+            grad_load(m).wait()
+
+        @pl.when(m + 1 < micro)
+        def _():
+            acts_load(after).wait()
+
+        for q in range(GROUPS):
+            @pl.when(jnp.logical_not(top))
+            def _():
+                relay(m, q).wait_recv()
+
+            chain(m, q, after)
+
+            @pl.when(pipe > 0)
+            def _():
+                relay(m, q).start()
+
+            if q == 0:
+                @pl.when(m == 1)
+                def _():
+                    hear(2)
+
+                @pl.when(m > 0)
+                def _():
+                    send_parts(m - 1)
+
+            @pl.when(jnp.logical_and(m == 0, top))
+            def _():
+                if q == 0:
+                    tiles_load.wait()
+                    blocks_load.wait()
+                build(q)
+                if q + 1 < GROUPS:
+                    start_slopes(q + 1)
+                if q == 0:
+                    hear(0)
+                    tell(1)
+                if q == GROUPS - 1:
+                    hear(1)
+                    tell(2)
 
         for r in range(rounds - 1):
             @pl.when(m == (ring * (r + 1) - 1) // slots + 2)
@@ -294,40 +357,47 @@
         return c
 
     lax.fori_loop(0, micro, step, 0)
+    for k in range(slots - 1, -1, -1):
+        project(micro - 1, GROUPS - 1, k)
+    send_parts(micro - 1)
     outer(rounds - 1)
     finish(rounds - 2)
+
+    def drain(m, c):
+        @pl.when(pipe > 0)
+        def _():
+            for q in range(GROUPS):
+                relay(m, q).wait_send()
+
+        for k in range(slots):
+            owner, copy = part_copy(m, k)
+
+            @pl.when(owner != me)
+            def _():
+                copy.wait_send()
+
+        return c
+
+    lax.fori_loop(0, micro, drain, 0)
+    for r in range(rounds):
+        for o in range(1, n_z):
+            z_copy(r, o).wait_send()
     finish(rounds - 1)
 
-    for r in range(rounds):
+    def widen(r):
         for o in range(1, ring):
             x_copy(r, o).wait_recv()
-    for n in range(slots * micro):
-        wide[pl.ds(n * half, half), :] = sk[n].astype(jnp.float32)
+        for n in range(r * ring, (r + 1) * ring):
+            wide[pl.ds(n * half, half), :] = sk[n].astype(jnp.float32)
+
+    for r in range(rounds):
+        widen(r)
     for k in range(slots):
         for i in range(half):
             sk_out[0, k, :, pl.ds(i * 2 * rank, 2 * rank)] = wide[
                 pl.ds(k * half + i, micro, stride=slots * half), :
             ]
-
-    def drain(m, c):
-        @pl.when(pipe > 0)
-        def _():
-            for q in range(GROUPS):
-                relay(m, q).wait_send()
-
-        for k in range(slots):
-            owner, copy = part_copy(m, k)
-
-            @pl.when(owner != me)
-            def _():
-                copy.wait_send()
-
-        return c
-
-    lax.fori_loop(0, micro, drain, 0)
     for r in range(rounds):
-        for o in range(1, n_z):
-            z_copy(r, o).wait_send()
         for o in range(1, ring):
             x_copy(r, o).wait_send()
 
@@ -345,7 +415,6 @@
     bf16, f32 = jnp.bfloat16, jnp.float32
     hbm = pl.BlockSpec(memory_space=pltpu.HBM)
     vmem = pl.BlockSpec(memory_space=pltpu.VMEM)
-    smem = pl.BlockSpec(memory_space=pltpu.SMEM)
     dma = pltpu.SemaphoreType.DMA
     gout, sk = pl.pallas_call(
         functools.partial(kernel, n_dp, n_pipe, n_tensor, 1.0 / math.sqrt(tokens * n_dp)),
@@ -353,9 +422,11 @@
             pltpu.VMEM((micro, tokens, width), bf16),
             pltpu.VMEM((1, slots, micro, rank * rank), f32),
         ),
-        in_specs=[smem, smem, hbm, hbm, hbm, hbm],
+        in_specs=[hbm] * 6,
         out_specs=(vmem, vmem),
         scratch_shapes=[
+            pltpu.SMEM(section_sizes.shape, jnp.int32),
+            pltpu.SMEM((slots, 1, n_tiles), jnp.int32),
             pltpu.VMEM((slots, micro, tokens, width), bf16),
             pltpu.VMEM((micro, tokens, width), bf16),
             pltpu.VMEM((slots, heads, hs, hs), bf16),
@@ -363,12 +434,14 @@
             pltpu.VMEM((slots, width, 2 * rank), bf16),
             pltpu.VMEM((slots, tokens, width), f32),
             pltpu.VMEM((slots, tokens, width), bf16),
+            pltpu.VMEM((slots, tokens, 2 * rank), f32),
             pltpu.VMEM((units, tokens, 2 * rank), bf16),
             pltpu.VMEM((rounds, ring - 1, tokens, 2 * rank), bf16),
             pltpu.VMEM((rounds, n_z, rank // 2, 2 * rank), bf16),
             pltpu.VMEM((units, rank // 2, 2 * rank), bf16),
             pltpu.VMEM((units * rank // 2, 2 * rank), f32),
-            dma((micro,)), dma((micro,)), dma((2,)),
+            dma((micro,)), dma((micro,)), dma((4,)),
+            pltpu.SemaphoreType.REGULAR((3,)), pltpu.SemaphoreType.REGULAR((3,)),
             dma((micro, GROUPS)), dma((micro, GROUPS)),
             dma((units,)), dma((rounds, ring - 1)),
             dma((rounds, n_z - 1)), dma((rounds, n_z - 1)),

time: 61.7 us -> 60.1 us (0.974)
  Pallas kernels: 61 us -> 59.4 us
    pallas_call x1, Pallas kernels: 59.8 us -> 58.3 us  [shards(): pl.pallas_call(functools.partial(kernel, n_dp, n_pipe, n_tensor, 1.0 / ma...]
where the time goes in v4:
time: 60.1 us
  Pallas kernels  59.4 us (99%)
  between operations  0.64 us (1%)
    pallas_call x1, Pallas kernels, shards(): pl.pallas_call(functools.partial(kernel, n_dp, n_pipe, n_tensor, 1.0 / ma...  58.3 us

profile of v4, /device:TPU:1, one launch (start us, length us, event | category | flops | bytes accessed | tf_op | source)
XLA Modules:
  0.0 60.1 jit_solution(16327394525179925294)
XLA Ops:
  0.6 58.3 %shard_map.77 = (bf16[8,64,1024]{2,1,0:T(8,128)(2,1)S(1)}, f32[1,3,8,4096]{3,2,1,0:T(8,128)S(1)}) custom-call(s32[4]{0:T(128)} %sizes_hbm.1, s32[3,1,8]{2,1,0:T(1,128)} %bitcast.1, bf16[8,64,1024]{2,1,0:T(8,128)(2,1)} %grad_hbm.1, bf16[1,3,8,64,1024]{4,3,2,1,0:T(8,128)(2,1)} %acts_hbm.1, bf16[1,3,8,128,128]{4,3,2,1,0:T(8,128)(2,1)} %mix_hbm.1, ...), custom_call_target="tpu_custom_call" | custom-call | tf_op jit(solution)/shard_map/pallas_call | solution.py:419
  58.9 1.1 %shard_map.78 = (bf16[1,8,64,1024]{3,2,1,0:T(8,128)(2,1)}, f32[1,3,8,4096]{3,2,1,0:T(8,128)}) custom-call(bf16[8,64,1024]{2,1,0:T(8,128)(2,1)S(1)} %get-tuple-element.4.gout, f32[1,3,8,4096]{3,2,1,0:T(8,128)S(1)} %get-tuple-element.5.sk), custom_call_target="tpu_custom_call" | custom-call | tf_op jit(solution)/shard_map/pallas_call | solution.py:457

commit v5 on v4

--- a/solution.py
+++ b/solution.py
@@ -33,7 +33,7 @@
     n_dp, n_pipe, n_tensor, scale,
     sizes_hbm, blocks_hbm, grad_hbm, acts_hbm, mix_hbm, tiles_hbm,
     gout, sk_out,
-    sizes, blocks, acts, gin, mix, tiles, dense, slope, delta, gathered, parts, red, zbuf, sk, wide,
+    sizes, blocks, acts, gin, mix, tiles, dense, slope, delta, gathered, parts, red, zbuf, sk, square,
     acts_sem, grad_sem, weight_sem, near_z, near_x,
     relay_send, relay_recv, part_send, part_recv, z_send, z_recv, x_send, x_recv,
 ):
@@ -198,14 +198,6 @@
             gout[m, :, pl.ds(h * hs, hs)] = g[h]
 
     def build(q):
-        r_in = lax.broadcasted_iota(jnp.int32, (2 * rank, 2 * rank), 0)
-        r_out = lax.broadcasted_iota(jnp.int32, (2 * rank, 2 * rank), 1)
-        moved = r_out - rank
-        from_row = jnp.where(
-            r_out < rank, r_out,
-            rank + jnp.where(moved < half, 2 * moved, 2 * (moved - half) + 1),
-        )
-        shuffle = jnp.where(r_in == from_row, 1.0, 0.0).astype(jnp.bfloat16)
         for k in range(slots):
             for b in group(q):
                 wanted = tensor * heads + b
@@ -215,8 +207,8 @@
                     hit = blocks[k, 0, j] == wanted
                     pick = jnp.where(hit, j, pick)
                     found = jnp.where(hit, 1, found)
-                block = jnp.dot(tiles[k, pick], shuffle, preferred_element_type=jnp.float32)
-                dense[k, pl.ds(b * hs, hs), :] = jnp.where(found == 1, block, 0.0).astype(jnp.bfloat16)
+                block = tiles[k, pick]
+                dense[k, pl.ds(b * hs, hs), :] = jnp.where(found == 1, block, jnp.zeros_like(block))
 
     def z_copy(r, o):
         return pltpu.make_async_remote_copy(
@@ -249,7 +241,10 @@
             x, y, (((0,), (0,)), ((), ())), precision=lax.Precision.HIGHEST,
             preferred_element_type=jnp.float32,
         )
-        out = jnp.where(low(half), t[rank : rank + half], t[rank + half :]) * scale
+        square[...] = t[rank:]
+        out = jnp.where(
+            low(half), square[pl.ds(0, half, stride=2), :], square[pl.ds(1, half, stride=2), :]
+        ) * scale
         zbuf[r, z] = jnp.where(lax.rem(n, slots) < sizes[pipe], out, 0.0).astype(jnp.bfloat16)
         for o in range(1, n_z):
             z_copy(r, o).start()
@@ -361,7 +356,6 @@
         project(micro - 1, GROUPS - 1, k)
     send_parts(micro - 1)
     outer(rounds - 1)
-    finish(rounds - 2)
 
     def drain(m, c):
         @pl.when(pipe > 0)
@@ -379,24 +373,23 @@
         return c
 
     lax.fori_loop(0, micro, drain, 0)
+    def unpack(r):
+        for o in range(1, ring):
+            x_copy(r, o).wait_recv()
+        for n in range(r * ring, (r + 1) * ring):
+            m, k = divmod(n, slots)
+            rows = pl.ds(k * half * micro + m, half, stride=micro)
+            sk_out[rows, :] = sk[n].astype(jnp.float32)
+
+    finish(rounds - 2)
+    for r in range(rounds - 2):
+        unpack(r)
     for r in range(rounds):
         for o in range(1, n_z):
             z_copy(r, o).wait_send()
     finish(rounds - 1)
-
-    def widen(r):
-        for o in range(1, ring):
-            x_copy(r, o).wait_recv()
-        for n in range(r * ring, (r + 1) * ring):
-            wide[pl.ds(n * half, half), :] = sk[n].astype(jnp.float32)
-
-    for r in range(rounds):
-        widen(r)
-    for k in range(slots):
-        for i in range(half):
-            sk_out[0, k, :, pl.ds(i * 2 * rank, 2 * rank)] = wide[
-                pl.ds(k * half + i, micro, stride=slots * half), :
-            ]
+    for r in range(rounds - 2, rounds):
+        unpack(r)
     for r in range(rounds):
         for o in range(1, ring):
             x_copy(r, o).wait_send()
@@ -420,7 +413,7 @@
         functools.partial(kernel, n_dp, n_pipe, n_tensor, 1.0 / math.sqrt(tokens * n_dp)),
         out_shape=(
             pltpu.VMEM((micro, tokens, width), bf16),
-            pltpu.VMEM((1, slots, micro, rank * rank), f32),
+            pltpu.VMEM((units * rank // 2, 2 * rank), f32),
         ),
         in_specs=[hbm] * 6,
         out_specs=(vmem, vmem),
@@ -439,7 +432,7 @@
             pltpu.VMEM((rounds, ring - 1, tokens, 2 * rank), bf16),
             pltpu.VMEM((rounds, n_z, rank // 2, 2 * rank), bf16),
             pltpu.VMEM((units, rank // 2, 2 * rank), bf16),
-            pltpu.VMEM((units * rank // 2, 2 * rank), f32),
+            pltpu.VMEM((rank, 2 * rank), f32),
             dma((micro,)), dma((micro,)), dma((4,)),
             pltpu.SemaphoreType.REGULAR((3,)), pltpu.SemaphoreType.REGULAR((3,)),
             dma((micro, GROUPS)), dma((micro, GROUPS)),
@@ -454,7 +447,7 @@
         pltpu.with_memory_space_constraint(x, pltpu.HBM)
         for x in (section_sizes, proj_blocks.transpose(1, 0, 2), grad_out, activations, mixing, proj_tiles)
     ])
-    return pl.pallas_call(
+    grads, sk = pl.pallas_call(
         store,
         out_shape=(
             jax.ShapeDtypeStruct((1,) + gout.shape, bf16), jax.ShapeDtypeStruct(sk.shape, f32),
@@ -464,6 +457,8 @@
         scratch_shapes=[dma((2,))],
         compiler_params=pltpu.CompilerParams(vmem_limit_bytes=1 << 20),
     )(*[pltpu.with_memory_space_constraint(x, pltpu.VMEM) for x in (gout, sk)])
+    sk = sk.reshape(slots, rank // 2, micro, 2 * rank).transpose(0, 2, 1, 3)
+    return grads, sk.reshape(1, slots, micro, rank * rank)
 
 
 def solution(mesh):

time: 60.1 us -> 59.9 us (level)
  no operation moved by 1% of the time
where the time goes in v5:
time: 59.9 us; the launch traced here: 59.8 us
  Pallas kernels  59.2 us (99%)
  between operations  0.64 us (1%)
    pallas_call x1, Pallas kernels, shards(): pl.pallas_call(functools.partial(kernel, n_dp, n_pipe, n_tensor, 1.0 / ma...  58.1 us

profile of v5, /device:TPU:1, one launch (start us, length us, event | category | flops | bytes accessed | tf_op | source)
XLA Modules:
  0.0 59.8 jit_solution(9699928640959546845)
XLA Ops:
  0.6 58.1 %shard_map.77 = (bf16[8,64,1024]{2,1,0:T(8,128)(2,1)S(1)}, f32[768,128]{1,0:T(8,128)S(1)}) custom-call(s32[4]{0:T(128)} %sizes_hbm.1, s32[3,1,8]{2,1,0:T(1,128)} %bitcast.6, bf16[8,64,1024]{2,1,0:T(8,128)(2,1)} %grad_hbm.1, bf16[1,3,8,64,1024]{4,3,2,1,0:T(8,128)(2,1)} %acts_hbm.1, bf16[1,3,8,128,128]{4,3,2,1,0:T(8,128)(2,1)} %mix_hbm.1, ...), custom_call_target="tpu_custom_call" | custom-call | tf_op jit(solution)/shard_map/pallas_call | solution.py:412
  58.7 1.1 %shard_map.78 = (bf16[1,8,64,1024]{3,2,1,0:T(8,128)(2,1)}, f32[768,128]{1,0:T(8,128)}) custom-call(bf16[8,64,1024]{2,1,0:T(8,128)(2,1)S(1)} %get-tuple-element.6.gout, f32[768,128]{1,0:T(8,128)S(1)} %get-tuple-element.7.sk), custom_call_target="tpu_custom_call" | custom-call | tf_op jit(solution)/shard_map/pallas_call | solution.py:450

commit v6 on v5

--- a/solution.py
+++ b/solution.py
@@ -16,6 +16,10 @@
     half = jnp.tanh(0.5 * value) * 0.5
     sig = 0.5 + half
     return sig * (1.0 + value * (0.5 - half))
+
+
+def far_first(size):
+    return sorted(range(1, size), key=lambda o: -min(o, size - o))
 
 
 def store(gout, sk, gout_hbm, sk_hbm, sem):
@@ -246,7 +250,7 @@
             low(half), square[pl.ds(0, half, stride=2), :], square[pl.ds(1, half, stride=2), :]
         ) * scale
         zbuf[r, z] = jnp.where(lax.rem(n, slots) < sizes[pipe], out, 0.0).astype(jnp.bfloat16)
-        for o in range(1, n_z):
+        for o in far_first(n_z):
             z_copy(r, o).start()
 
     def finish(r):
@@ -256,7 +260,7 @@
         for zz in range(1, n_z):
             total = total + zbuf[r, zz].astype(jnp.float32)
         sk[r * ring + me] = total.astype(jnp.bfloat16)
-        for o in range(1, ring):
+        for o in far_first(ring):
             x_copy(r, o).start()
 
     mix_load.wait()

time: 59.9 us -> 59.2 us (0.988)
  Pallas kernels: 59.2 us -> 58.5 us
    pallas_call x1, Pallas kernels: 58.1 us -> 57.4 us  [shards(): pl.pallas_call(functools.partial(kernel, n_dp, n_pipe, n_tensor, 1.0 / ma...]
where the time goes in v6:
time: 59.2 us; the launch traced here: 59.1 us
  Pallas kernels  58.5 us (99%)
  between operations  0.64 us (1%)
    pallas_call x1, Pallas kernels, shards(): pl.pallas_call(functools.partial(kernel, n_dp, n_pipe, n_tensor, 1.0 / ma...  57.4 us

profile of v6, /device:TPU:1, one launch (start us, length us, event | category | flops | bytes accessed | tf_op | source)
XLA Modules:
  0.0 59.1 jit_solution(8551636420049297857)
XLA Ops:
  0.6 57.4 %shard_map.77 = (bf16[8,64,1024]{2,1,0:T(8,128)(2,1)S(1)}, f32[768,128]{1,0:T(8,128)S(1)}) custom-call(s32[4]{0:T(128)} %sizes_hbm.1, s32[3,1,8]{2,1,0:T(1,128)} %bitcast.6, bf16[8,64,1024]{2,1,0:T(8,128)(2,1)} %grad_hbm.1, bf16[1,3,8,64,1024]{4,3,2,1,0:T(8,128)(2,1)} %acts_hbm.1, bf16[1,3,8,128,128]{4,3,2,1,0:T(8,128)(2,1)} %mix_hbm.1, ...), custom_call_target="tpu_custom_call" | custom-call | tf_op jit(solution)/shard_map/pallas_call | solution.py:416
  58.0 1.1 %shard_map.78 = (bf16[1,8,64,1024]{3,2,1,0:T(8,128)(2,1)}, f32[768,128]{1,0:T(8,128)}) custom-call(bf16[8,64,1024]{2,1,0:T(8,128)(2,1)S(1)} %get-tuple-element.6.gout, f32[768,128]{1,0:T(8,128)S(1)} %get-tuple-element.7.sk), custom_call_target="tpu_custom_call" | custom-call | tf_op jit(solution)/shard_map/pallas_call | solution.py:454
